TPU v7x, 32 devices: a whole 2x2x4 slice. The times are simulated.
32 devices in a mesh: sweep: 2 (over x), recv: 16 (over z, y, core).
Axes of the slice: x: 2, y: 2, z: 4, core: 2. Of those that a mesh axis runs over, the one named last changes fastest.
Arguments:
- records: bfloat16 [16, 1024, 4096], P('sweep', 'recv'), may hold values from -6 to 6
- pilots: bfloat16 [16, 3968], replicated, may hold values from -0.09375 to 0.09375
- hadamard: int32 [16, 16], replicated, may hold values from -1 to 1, as said below
- code_vibrator: int32 [16], replicated, may hold values from 0 to 15, each once
- owner_map: int32 [1024], P('recv'), may hold values from 0 to 15
- live_mask: int32 [1024], P('recv'), may hold values 0 or 1
- filters: bfloat16 [16, 128, 128], P('sweep'), may hold values from -0.5 to 0.5
- targets: bfloat16 [16, 1024, 128], P('sweep', 'recv'), may hold values from -6 to 6
Outputs:
- responses: float32 [16, 1024, 128], P('sweep', 'recv')
- gradient: float32 [16, 128, 128], P('sweep', 'recv')
Inputs may be any that keep to these rules, and one draw needn't show every extreme that they name: hadamard transposed times hadamard is 16 times the identity. `code_vibrator`: every vibrator belongs to exactly one code.
All inputs are finite; a program needn't handle non-finite values. No bound on the sum of `live_mask` on one device may be relied on, other than what follows from the above.
Results may differ from a plain program's by a relative error of at most 0.0085.
Values may be sent and summed in bfloat16 or wider, within the bound.
No kernel may reach another device: no remote copies, remote signals or barrier semaphores. Data moves between devices by JAX's collectives and lax.ppermute only.
A program may use at most 64 MiB of HBM per device.

v0:
```python
import math

import jax
import jax.numpy as jnp
from jax import lax
from jax.sharding import PartitionSpec as P


def toeplitz(sweep_pilot, samples, lagcount):
    padding = jnp.zeros((samples + 1 - sweep_pilot.shape[0],), sweep_pilot.dtype)
    extended = jnp.concatenate([sweep_pilot, padding])
    return jnp.tile(extended, lagcount)[: lagcount * samples].reshape(lagcount, samples)


def correlate_split(combined, sweep_pilot, samples, lagcount):
    upper = combined.astype(jnp.bfloat16)
    lower = (combined - upper.astype(jnp.float32)).astype(jnp.bfloat16)
    paired = jnp.concatenate([upper, lower], axis=0)
    toe_rows = toeplitz(sweep_pilot, samples, lagcount)
    lagged = lax.dot_general(
        paired, toe_rows, (((1,), (1,)), ((), ())), preferred_element_type=jnp.float32
    )
    half = combined.shape[0]
    return lagged[:half] + lagged[half:]


def local(records, pilots, hadamard, code_vibrator, owner_map, live_mask, filters, targets):
    sweeps = lax.axis_size("sweep")
    codes = hadamard.shape[1]
    held_sweeps = records.shape[0]
    channels = records.shape[1]
    samples = records.shape[2]
    lagcount = filters.shape[1]
    owned_codes = filters.shape[0]
    first_code = lax.axis_index("sweep") * owned_codes
    code_norm = 1.0 / math.sqrt(codes)
    onehot = (code_vibrator[:, None] == jnp.arange(codes, dtype=jnp.int32)[None, :]).astype(
        jnp.bfloat16
    )
    code_pilot = jnp.dot(onehot, pilots, preferred_element_type=jnp.float32).astype(jnp.bfloat16)
    blocks = records.reshape(held_sweeps, sweeps, channels // sweeps, samples)
    gathered = lax.all_to_all(blocks, "sweep", split_axis=1, concat_axis=0, tiled=True)
    gathered = gathered.reshape(codes, channels // sweeps, samples)
    decoded_raw = jnp.einsum(
        "sc,srt->crt", hadamard.astype(jnp.bfloat16), gathered, preferred_element_type=jnp.float32
    )

    def column(operands):
        decoded_line, sweep_pilot = operands
        return code_norm * correlate_split(decoded_line, sweep_pilot, samples, lagcount)

    all_codes = lax.map(column, (decoded_raw, code_pilot)).astype(jnp.bfloat16)
    decoded = lax.all_to_all(all_codes, "sweep", split_axis=0, concat_axis=1, tiled=True)
    col_vibs = lax.dynamic_slice_in_dim(code_vibrator, first_code, owned_codes, 0)
    responses = jnp.einsum("crl,clm->crm", decoded, filters, preferred_element_type=jnp.float32)
    owned = (owner_map[None, :] == col_vibs[:, None]).astype(jnp.float32)
    weight = live_mask.astype(jnp.float32)[None, :] * (0.25 + owned)
    residual = (weight[:, :, None] * (responses - targets.astype(jnp.float32))).astype(jnp.bfloat16)
    factor = 1.0 / math.sqrt(channels * lax.axis_size("recv"))
    local_grad = (
        jnp.einsum("crl,crm->clm", decoded, residual, preferred_element_type=jnp.float32) * factor
    )
    summed = lax.psum(local_grad, "recv")
    share_rows = lagcount // lax.axis_size("recv")
    gradient = lax.dynamic_slice_in_dim(summed, lax.axis_index("recv") * share_rows, share_rows, 1)
    return (responses, gradient)


def solution(mesh):
    in_specs = (
        P("sweep", "recv", None),
        P(),
        P(),
        P(),
        P("recv"),
        P("recv"),
        P("sweep", None, None),
        P("sweep", "recv", None),
    )
    out_specs = (P("sweep", "recv", None), P("sweep", "recv", None))
    return jax.shard_map(local, mesh=mesh, in_specs=in_specs, out_specs=out_specs, check_vma=False)
```

profile of v0, /device:TPU:0, one launch (start us, length us, event | category | flops | bytes accessed | tf_op | source)
XLA Modules:
  0.0 284.5 jit_solution(12930026134246366207)
XLA Ops:
  7.2 6.5 %copy.18 = bf16[8,64,4096]{2,0,1:T(8,128)(2,1)} copy(bf16[8,64,4096]{2,1,0:T(8,128)(2,1)} %param.10) | data formatting | bytes 8388608 | tf_op args[0]
  13.7 5.8 %all-to-all-start = ((bf16[8,2,32,4096]{3,0,2,1:T(8,128)(2,1)}), bf16[8,2,32,4096]{3,0,2,1:T(8,128)(2,1)}, u32[]{:S(2)}, u32[]{:S(2)}) async-start(bf16[8,2,32,4096]{3,0,2,1:T(8,128)(2,1)} %bitcast.43), calls=%async_computation | async-start | bytes 8388608 | tf_op jit(solution)/shard_map/all_to_all | solution.py:42
  19.8 48.5 %all-to-all-done = bf16[8,2,32,4096]{3,0,2,1:T(8,128)(2,1)} async-done(((bf16[8,2,32,4096]{3,0,2,1:T(8,128)(2,1)}), bf16[8,2,32,4096]{3,0,2,1:T(8,128)(2,1)}, u32[]{:S(2)}, u32[]{:S(2)}) %all-to-all-start) | async-done | bytes 4194336 | tf_op jit(solution)/shard_map/all_to_all | solution.py:42
  68.3 6.7 %fusion.9 = f32[16,32,4096]{2,0,1:T(8,128)} fusion(s32[16,16]{1,0:T(8,128)S(1)} %copy-done.4, bf16[8,2,32,4096]{3,0,2,1:T(8,128)(2,1)} %all-to-all-done), kind=kOutput, calls=%fused_computation.15 | convolution fusion | flops 67109120 | bytes 12583936 | tf_op jit(solution)/shard_map/sc,srt->crt/dot_general | solution.py:44
  75.0 100.5 %while.10 = (s32[]{:T(128)}, bf16[16,32,128]{2,1,0:T(8,128)(2,1)}, f32[16,32,4096]{2,0,1:T(8,128)}, bf16[16,3968]{1,0:T(8,128)(2,1)S(1)}, s32[]{:T(128)}, /*index=5*/bf16[]{:T(256)}) while((s32[]{:T(128)}, bf16[16,32,128]{2,1,0:T(8,128)(2,1)}, f32[16,32,4096]{2,0,1:T(8,128)}, bf16[16,3968]{1,0:T(8,128)(2,1)S(1)}, s32[]{:T(128)}, ...), condition=%wide.region_1.2_spmd, body=%wide.region_0.1_spmd.sunk | while | flops 68689920 | bytes 11657811 | solution.py:52
  75.0 2.7 constant_dynamic-slice_fusion.3
  78.5 1.2 tile.12
  80.7 0.6 fusion.30
  81.3 2.7 constant_dynamic-slice_fusion.3
  84.8 1.2 tile.12
  87.0 0.6 fusion.30
  87.6 2.7 constant_dynamic-slice_fusion.3
  91.1 1.2 tile.12
  93.3 0.6 fusion.30
  93.9 2.7 constant_dynamic-slice_fusion.3
  97.3 1.2 tile.12
  99.6 0.6 fusion.30
  100.2 2.7 constant_dynamic-slice_fusion.3
  103.6 1.2 tile.12
  105.8 0.6 fusion.30
  106.4 2.7 constant_dynamic-slice_fusion.3
  109.9 1.2 tile.12
  112.1 0.6 fusion.30
  112.7 2.7 constant_dynamic-slice_fusion.3
  116.2 1.2 tile.12
  119.0 2.7 constant_dynamic-slice_fusion.3
  122.4 1.2 tile.12
  125.3 2.7 constant_dynamic-slice_fusion.3
  128.7 1.2 tile.12
  131.6 2.7 constant_dynamic-slice_fusion.3
  135.0 1.2 tile.12
  137.8 2.7 constant_dynamic-slice_fusion.3
  141.3 1.2 tile.12
  144.1 2.7 constant_dynamic-slice_fusion.3
  147.6 1.2 tile.12
  150.4 2.7 constant_dynamic-slice_fusion.3
  153.8 1.2 tile.12
  156.7 2.7 constant_dynamic-slice_fusion.3
  160.1 1.2 tile.12
  162.9 2.7 constant_dynamic-slice_fusion.3
  166.4 1.2 tile.12
  169.2 2.7 constant_dynamic-slice_fusion.3
  172.7 1.2 tile.12
  175.5 3.4 %all-to-all-start.1 = ((bf16[16,32,128]{2,1,0:T(8,128)(2,1)}), bf16[16,32,128]{2,1,0:T(8,128)(2,1)S(1)}, u32[]{:S(2)}, u32[]{:S(2)}) async-start(bf16[16,32,128]{2,1,0:T(8,128)(2,1)} %get-tuple-element.24), calls=%async_computation.1 | async-start | bytes 262144 | tf_op jit(solution)/shard_map/all_to_all | solution.py:53
  179.0 4.3 %all-to-all-done.1 = bf16[16,32,128]{2,1,0:T(8,128)(2,1)S(1)} async-done(((bf16[16,32,128]{2,1,0:T(8,128)(2,1)}), bf16[16,32,128]{2,1,0:T(8,128)(2,1)S(1)}, u32[]{:S(2)}, u32[]{:S(2)}) %all-to-all-start.1) | async-done | bytes 131104 | tf_op jit(solution)/shard_map/all_to_all | solution.py:53
  183.6 1.2 convolution_multiply_fusion
  184.8 91.5 %all-reduce.3.cloned.1.call-done = f32[8,128,128]{2,1,0:T(8,128)} async-done(((f32[8,128,128]{2,1,0:T(8,128)}), f32[8,128,128]{2,1,0:T(8,128)}) %all-reduce.3.cloned.1.call-update) | async-done | bytes 524304 | tf_op jit(solution)/shard_map/psum | solution.py:63
  276.3 1.4 constant_dynamic-slice_fusion.1
  (163 shorter events, 35.3 us)
Async XLA Ops:
  7.2 176.2 %copy-start = (bf16[8,128,128]{2,1,0:T(8,128)(2,1)S(1)}, bf16[8,128,128]{2,1,0:T(8,128)(2,1)}, u32[]{:S(2)}) copy-start(bf16[8,128,128]{2,1,0:T(8,128)(2,1)} %param.16) | copy-start | bytes 786436
  13.7 5.8 %copy-start.7 = (s32[64]{0:T(128)S(1)}, s32[64]{0:T(128)}, u32[]{:S(2)}) copy-start(s32[64]{0:T(128)} %param.15) | copy-start | bytes 772
  13.7 5.8 %copy-start.5 = (s32[16]{0:T(128)S(1)}, s32[16]{0:T(128)}, u32[]{:S(2)}) copy-start(s32[16]{0:T(128)} %param.13) | copy-start | bytes 196
  13.7 5.9 %copy-start.3 = (bf16[16,3968]{1,0:T(8,128)(2,1)S(1)}, bf16[16,3968]{1,0:T(8,128)(2,1)}, u32[]{:S(2)}) copy-start(bf16[16,3968]{1,0:T(8,128)(2,1)} %param.11) | copy-start | bytes 380932
  13.7 54.7 %copy-start.4 = (s32[16,16]{1,0:T(8,128)S(1)}, s32[16,16]{1,0:T(8,128)}, u32[]{:S(2)}) copy-start(s32[16,16]{1,0:T(8,128)} %param.12) | copy-start | bytes 3076
  13.7 54.6 %all-to-all-start = ((bf16[8,2,32,4096]{3,0,2,1:T(8,128)(2,1)}), bf16[8,2,32,4096]{3,0,2,1:T(8,128)(2,1)}, u32[]{:S(2)}, u32[]{:S(2)}) async-start(bf16[8,2,32,4096]{3,0,2,1:T(8,128)(2,1)} %bitcast.43), calls=%async_computation | async-start | bytes 8388608 | tf_op jit(solution)/shard_map/all_to_all | solution.py:42
  75.0 103.9 %copy-start.6 = (s32[64]{0:T(128)S(1)}, s32[64]{0:T(128)}, u32[]{:S(2)}) copy-start(s32[64]{0:T(128)} %param.14) | copy-start | bytes 772
  75.0 108.5 %copy-start.2 = (bf16[8,64,128]{2,1,0:T(8,128)(2,1)S(1)}, bf16[8,64,128]{2,1,0:T(8,128)(2,1)}, u32[]{:S(2)}) copy-start(bf16[8,64,128]{2,1,0:T(8,128)(2,1)} %param.17) | copy-start | bytes 393220
  175.5 7.8 %all-to-all-start.1 = ((bf16[16,32,128]{2,1,0:T(8,128)(2,1)}), bf16[16,32,128]{2,1,0:T(8,128)(2,1)S(1)}, u32[]{:S(2)}, u32[]{:S(2)}) async-start(bf16[16,32,128]{2,1,0:T(8,128)(2,1)} %get-tuple-element.24), calls=%async_computation.1 | async-start | bytes 262144 | tf_op jit(solution)/shard_map/all_to_all | solution.py:53
  178.9 97.4 %all-reduce.3.cloned.1.call-start = ((), (), s32[]{:S(2)}) async-start(), calls=%async_computation.2 | async-start | bytes 1048576 | tf_op jit(solution)/shard_map/psum | solution.py:63
  183.6 94.1 %copy-start.1 = (f32[8,64,128]{2,1,0:T(8,128)}, f32[8,64,128]{2,1,0:T(8,128)S(1)}, u32[]{:S(2)}) copy-start(f32[8,64,128]{2,1,0:T(8,128)S(1)} %fusion.16) | copy-start | bytes 786436
Sparse Core Ops, SparseCore 0:
  184.9 91.3 all-reduce.2
where the time goes:
time: 285 us; the launch traced here: 284 us
  waiting for transfers between devices  144 us (51%)
  local copies, waits for them, and re-layouts  85.3 us (30%)
  matrix products  15.9 us (6%)
  other arithmetic  14.5 us (5%)
  between operations  14.1 us (5%)
  starting transfers between devices  9.19 us (3%)
    psum x1, waiting for transfers between devices, local(): summed = lax.psum(local_grad, 'recv')  91.5 us
    dynamic_slice x48, local copies, waits for them, and re-layouts, local(): all_codes = lax.map(column, (decoded_raw, code_pilot)).astype(jnp.bfloat16)  48.6 us
    all_to_all x1, waiting for transfers between devices, local(): lax.all_to_all(blocks, 'sweep', split_axis=1, concat_axis=0, tiled=True)  48.5 us
    another operation x32, local copies, waits for them, and re-layouts, toeplitz(): jnp.tile(extended, lagcount)[:lagcount * samples].reshape(lagcount, samples)  19.6 us
    dynamic_update_slice x16, other arithmetic, local(): all_codes = lax.map(column, (decoded_raw, code_pilot)).astype(jnp.bfloat16)  9.76 us
    reshape x16, local copies, waits for them, and re-layouts, toeplitz(): jnp.tile(extended, lagcount)[:lagcount * samples].reshape(lagcount, samples)  7.9 us
    dot_general x16, matrix products, correlate_split(): lax.dot_general(paired, toe_rows, (((1,), (1,)), ((), ())), preferred_ele...  7.67 us
    dot_general x1, matrix products, local(): jnp.einsum('sc,srt->crt', hadamard.astype(jnp.bfloat16), gathered, prefer...  6.7 us
  transfers between devices with their start and end apart: 3, of which 3 were waited for; matrix products, arithmetic and copies ran while one was open for 0% of the time, Pallas kernels for 0%

commit v1 on v0

v1 whole, which is shorter than its diff:
```python
import functools
import math

import jax
import jax.numpy as jnp
from jax import lax
from jax.experimental import pallas as pl
from jax.experimental.pallas import tpu as pltpu
from jax.sharding import PartitionSpec as P

BF16 = jnp.bfloat16
F32 = jnp.float32
SMEM = pl.BlockSpec(memory_space=pltpu.SMEM)
VMEM = pl.BlockSpec(memory_space=pltpu.VMEM)
ANY = pl.BlockSpec(memory_space=pl.ANY)
SKEW = 16


def iota(shape, axis):
    return lax.broadcasted_iota(jnp.int32, shape, axis)


def decode_kernel(vib, hadamard, pilots, records, out, held, sems, mix, pilot_rows, skewed, total, *, step, width):
    sweeps, channels, samples = records.shape
    owned, _, lags = out.shape
    block = mix.shape[1] // sweeps
    shift = block.bit_length() - 1
    length = pilots.shape[1]
    chunks = samples // width
    groups = lax.axis_size("sweep")
    mine = lax.axis_index("sweep")
    group = lax.rem(mine + step, groups)
    first_sweep = mine * sweeps
    first_code = group * owned

    def fetch(k):
        cols = pl.ds(pl.multiple_of(k * width, width), width)
        return pltpu.make_async_copy(records.at[:, :, cols], held.at[:, :, cols], sems.at[k])

    for k in range(chunks):
        fetch(k).start()
    signs = hadamard[...].astype(F32).astype(BF16)
    all_sweeps, codes = hadamard.shape
    rows, cols = mix.shape
    pick_code = (iota((rows, codes), 1) == first_code + (iota((rows, codes), 0) >> shift)).astype(F32).astype(BF16)
    pick_sweep = (iota((all_sweeps, cols), 0) == first_sweep + (iota((all_sweeps, cols), 1) >> shift)).astype(F32).astype(BF16)
    by_code = lax.dot_general(pick_code, signs, (((1,), (1,)), ((), ())), preferred_element_type=F32).astype(BF16)
    spread = jnp.dot(by_code, pick_sweep, preferred_element_type=F32)
    same = (iota((rows, cols), 0) & (block - 1)) == (iota((rows, cols), 1) & (block - 1))
    mix[...] = jnp.where(same, spread, 0.0).astype(BF16)
    pilot_rows[:, :length] = pilots[...].astype(F32)
    pilot_rows[:, length:] = jnp.zeros((pilots.shape[0], samples - length), F32)
    for c in range(owned):
        row = pilot_rows[pl.ds(vib[first_code + c], 1), :]
        wide = jnp.broadcast_to(row, (SKEW, samples))
        skewed[c, :, :lags] = jnp.zeros((SKEW, lags), BF16)
        skewed[c, :, lags:] = pltpu.roll(wide, 0, 1, stride=1, stride_axis=0).astype(BF16)
    total[...] = jnp.zeros_like(total)

    def chunk(k, carry):
        fetch(k).wait()
        start = pl.multiple_of(k * width, width)
        mixed = []
        for h in range(channels // block):
            traces = held[:, h * block : (h + 1) * block, pl.ds(start, width)].reshape(cols, width)
            mixed.append(jnp.dot(mix[...], traces, preferred_element_type=F32).astype(BF16))
        for c in range(owned):
            lines = jnp.concatenate([m[c * block : (c + 1) * block] for m in mixed], axis=0)
            window = skewed[c, :, pl.ds(start, width + lags)]
            shifts = [window[:, lags - j : lags - j + width] for j in range(0, lags, SKEW)]
            total[c] += lax.dot_general(
                lines, jnp.concatenate(shifts, axis=0), (((1,), (1,)), ((), ())), preferred_element_type=F32
            )
        return carry

    lax.fori_loop(0, chunks, chunk, 0)
    out[...] = total[...].astype(out.dtype)


def decode(vib, hadamard, pilots, records, owned, lags, step, dtype):
    sweeps, channels, samples = records.shape
    block = min(channels, 256 // sweeps)
    width = 1024
    return pl.pallas_call(
        functools.partial(decode_kernel, step=step, width=width),
        out_shape=jax.ShapeDtypeStruct((owned, channels, lags), dtype),
        in_specs=[SMEM, VMEM, VMEM, ANY],
        out_specs=VMEM,
        scratch_shapes=[
            pltpu.VMEM((sweeps, channels, samples), BF16),
            pltpu.SemaphoreType.DMA((samples // width,)),
            pltpu.VMEM((owned * block, sweeps * block), BF16),
            pltpu.VMEM((pilots.shape[0], samples), F32),
            pltpu.VMEM((owned, SKEW, lags + samples), BF16),
            pltpu.VMEM((owned, channels, lags), F32),
        ],
        cost_estimate=pl.CostEstimate(flops=8 * 10**9, bytes_accessed=records.size * 2, transcendentals=0),
        name=f"decode_{step}",
    )(vib, hadamard, pilots, records)


def tail_kernel(vib, owner, live, own, *refs, parts, radix, norm, factor):
    others, (filters, targets, responses, keep), sends, terms = refs[:parts], refs[parts : parts + 4], refs[parts + 4 : -1], refs[-1]
    owned, channels, lags = own.shape
    first_code = lax.axis_index("sweep") * owned
    digit = lax.rem(lax.axis_index("recv"), radix)
    eye = iota((channels, channels), 0) == iota((channels, channels), 1)

    def column(row):
        return jnp.sum(jnp.where(eye, jnp.broadcast_to(row.astype(F32), (channels, channels)), 0.0), axis=1, keepdims=True)

    owner_col = column(owner[...])
    live_col = column(live[...])
    shares, _, share_rows, _ = terms.shape
    for c in range(owned):
        partial = own[c]
        for other in others:
            partial = partial + other[c].astype(F32)
        decoded = (norm * partial).astype(BF16)
        response = jnp.dot(decoded, filters[c], preferred_element_type=F32)
        responses[c] = response
        match = (owner_col == vib[first_code + c].astype(F32)).astype(F32)
        weight = live_col * (0.25 + match)
        residual = (weight * (response - targets[c].astype(F32))).astype(BF16)
        grad = factor * lax.dot_general(decoded, residual, (((0,), (0,)), ((), ())), preferred_element_type=F32)
        for d in range(shares):
            terms[d, c] = grad[d * share_rows : (d + 1) * share_rows]
    for hi in range(shares // radix):
        keep[hi] = terms[hi * radix + digit]
        for k, send in enumerate(sends):
            send[hi] = terms[hi * radix + peer(digit, k + 1, radix)].astype(BF16)


def peer(digit, k, radix):
    if radix & (radix - 1) == 0:
        return digit ^ k
    return lax.rem(digit + k, radix) if not isinstance(digit, int) else (digit + k) % radix


def radices(size):
    parts = []
    for want in (2, 4):
        if size % want == 0 and size > 1:
            parts.append(want)
            size //= want
    while size > 1:
        f = next(q for q in (2, 3, 5, 7, size) if size % q == 0)
        parts.append(f)
        size //= f
    return parts or [1]


def exchange(values, stride, radix, size):
    got = []
    for k, value in enumerate(values):
        pairs = []
        for i in range(size):
            d = i // stride % radix
            pairs.append((i, i + (peer(d, k + 1, radix) - d) * stride))
        got.append(lax.ppermute(value, "recv", pairs))
    return got


def local(records, pilots, hadamard, code_vibrator, owner_map, live_mask, filters, targets):
    groups = lax.axis_size("sweep")
    size = lax.axis_size("recv")
    codes = hadamard.shape[1]
    owned, lags, _ = filters.shape
    channels = records.shape[1]
    received = []
    for step in range(1, groups):
        part = decode(code_vibrator, hadamard, pilots, records, owned, lags, step, BF16)
        received.append(lax.ppermute(part, "sweep", [(i, (i + step) % groups) for i in range(groups)]))
    own = decode(code_vibrator, hadamard, pilots, records, owned, lags, 0, F32)
    steps = radices(size)
    share_rows = lags // size
    piece = (size // steps[0], owned, share_rows, lags)
    outs = pl.pallas_call(
        functools.partial(
            tail_kernel,
            parts=len(received),
            radix=steps[0],
            norm=1.0 / math.sqrt(codes),
            factor=1.0 / math.sqrt(channels * size),
        ),
        out_shape=[jax.ShapeDtypeStruct((owned, channels, lags), F32), jax.ShapeDtypeStruct(piece, F32)]
        + [jax.ShapeDtypeStruct(piece, BF16)] * (steps[0] - 1),
        in_specs=[SMEM] + [VMEM] * (5 + len(received)),
        out_specs=[VMEM] * (1 + steps[0]),
        scratch_shapes=[pltpu.VMEM((size, owned, share_rows, lags), F32)],
        name="tail",
    )(code_vibrator, owner_map.reshape(1, channels), live_mask.reshape(1, channels), own, *received, filters, targets)
    responses, held, sends = outs[0], outs[1], outs[2:]
    me = lax.axis_index("recv")
    stride = 1
    for radix, after in zip(steps, steps[1:] + [None]):
        for got in exchange(sends, stride, radix, size):
            held = held + got.astype(F32)
        stride *= radix
        if after is None:
            break
        digit = me // stride % after
        grid = held.reshape((held.shape[0] // after, after) + held.shape[1:])
        sends = [lax.dynamic_index_in_dim(grid, peer(digit, k, after), 1, keepdims=False).astype(BF16) for k in range(1, after)]
        held = lax.dynamic_index_in_dim(grid, digit, 1, keepdims=False)
    return (responses, held[0])


def solution(mesh):
    in_specs = (
        P("sweep", "recv", None),
        P(),
        P(),
        P(),
        P("recv"),
        P("recv"),
        P("sweep", None, None),
        P("sweep", "recv", None),
    )
    out_specs = (P("sweep", "recv", None), P("sweep", "recv", None))
    return jax.shard_map(local, mesh=mesh, in_specs=in_specs, out_specs=out_specs, check_vma=False)
```

time: 285 us -> 38.1 us (0.13)
  waiting for transfers between devices: 144 us -> 7.01 us
  local copies, waits for them, and re-layouts: 85.3 us -> 0.68 us
  Pallas kernels: 0 us -> 18.7 us
  matrix products: 15.9 us -> 0 us
  between operations: 14.1 us -> 0.69 us
  other arithmetic: 14.5 us -> 1.61 us
    psum x1 -> x0, waiting for transfers between devices: 91.5 us -> none  [local(): summed = lax.psum(local_grad, 'recv')]
    all_to_all x2 -> x0, waiting for transfers between devices: 52.8 us -> none  [the longest x1 48.5 us: local(): lax.all_to_all(blocks, 'sweep', split_axis=1, concat_axis=0, tiled=True)]
    dynamic_slice x50 -> x0, local copies, waits for them, and re-layouts: 50 us -> none  [the longest x48 48.6 us: local(): all_codes = lax.map(column, (decoded_raw, code_pilot)).astype(jnp.bfloat16)]
    another operation x32 -> x0, local copies, waits for them, and re-layouts: 19.6 us -> none  [toeplitz(): jnp.tile(extended, lagcount)[:lagcount * samples].reshape(lagcount, samples)]
    pallas_call x0 -> x3, Pallas kernels: none -> 18.7 us  [the longest x2 15.5 us: decode(): pl.pallas_call(functools.partial(decode_kernel, step=step, width=width),...]
    dot_general x20 -> x0, matrix products: 15.9 us -> none  [the longest x16 7.67 us: correlate_split(): lax.dot_general(paired, toe_rows, (((1,), (1,)), ((), ())), preferred_ele...]
    dynamic_update_slice x16 -> x0, other arithmetic: 9.76 us -> none  [local(): all_codes = lax.map(column, (decoded_raw, code_pilot)).astype(jnp.bfloat16)]
    ppermute x0 -> x6, starting transfers between devices: none -> 9.24 us  [the longest x5 6.21 us: exchange(): got.append(lax.ppermute(value, 'recv', pairs))]
  transfers between devices with their start and end apart: 3 -> 6, of which waited for: 3 -> 5; matrix products, arithmetic and copies ran while one was open for 0% -> 0% of each run, Pallas kernels for 0% -> 20%
where the time goes in v1:
time: 38.1 us; the launch traced here: 37.9 us
  Pallas kernels  18.7 us (49%)
  starting transfers between devices  9.24 us (24%)
  waiting for transfers between devices  7.01 us (18%)
  other arithmetic  1.61 us (4%)
  between operations  0.69 us (2%)
  local copies, waits for them, and re-layouts  0.68 us (2%)
    pallas_call x2, Pallas kernels, decode(): pl.pallas_call(functools.partial(decode_kernel, step=step, width=width),...  15.5 us
    ppermute x5, waiting for transfers between devices, exchange(): got.append(lax.ppermute(value, 'recv', pairs))  7.01 us
    ppermute x5, starting transfers between devices, exchange(): got.append(lax.ppermute(value, 'recv', pairs))  6.21 us
    pallas_call x1, Pallas kernels, local(): pl.pallas_call(functools.partial(tail_kernel, parts=len(received), radix=...  3.21 us
    ppermute x1, starting transfers between devices, local(): lax.ppermute(part, 'sweep', [(i, (i + step) % groups) for i in range(grou...  3.03 us
    add x2, other arithmetic, local(): held = held + got.astype(F32)  0.99 us
  transfers between devices with their start and end apart: 6, of which 5 were waited for; matrix products, arithmetic and copies ran while one was open for 0% of the time, Pallas kernels for 20%

profile of v1, /device:TPU:0, one launch (start us, length us, event | category | flops | bytes accessed | tf_op | source)
XLA Modules:
  0.0 37.9 jit_solution(18079329502608805187)
XLA Ops:
  0.6 7.7 %decode_1.1 = bf16[8,64,128]{2,1,0:T(8,128)(2,1)} custom-call(s32[16]{0:T(128)} %vib.5, s32[16,16]{1,0:T(8,128)} %hadamard.3, bf16[16,3968]{1,0:T(8,128)(2,1)} %pilots.3, bf16[8,64,4096]{2,1,0:T(8,128)(2,1)} %records.3), custom_call_target="tpu_custom_call" | custom-call | flops 8000000000 | bytes 4194304 | tf_op jit(solution)/shard_map/decode_1/pallas_call | solution.py:84
  8.3 3.0 %collective-permute-start = (bf16[8,64,128]{2,1,0:T(8,128)(2,1)}, bf16[8,64,128]{2,1,0:T(8,128)(2,1)S(1)}, u32[]{:S(2)}, u32[]{:S(2)}) collective-permute-start(bf16[8,64,128]{2,1,0:T(8,128)(2,1)} %decode_1.1), channel_id=1, source_target_pairs={{0,16},{16,0},{1,17},{17,1},{2,18},{18,2},{3,19},{19,3},{4,20},{20... | collective-permute-start | bytes 393224 | tf_op jit(solution)/shard_map/ppermute | solution.py:173
  11.4 7.7 %decode_0.1.own = f32[8,64,128]{2,1,0:T(8,128)} custom-call(s32[16]{0:T(128)} %vib.5, s32[16,16]{1,0:T(8,128)} %hadamard.3, bf16[16,3968]{1,0:T(8,128)(2,1)} %pilots.3, bf16[8,64,4096]{2,1,0:T(8,128)(2,1)} %records.3), custom_call_target="tpu_custom_call" | custom-call | flops 8000000000 | bytes 4194304 | tf_op jit(solution)/shard_map/decode_0/pallas_call | solution.py:84
  19.1 0.0 collective-permute-done.refs_0_
  19.1 0.0 copy-start
  19.1 0.6 %copy-done = bf16[8,64,128]{2,1,0:T(8,128)(2,1)} copy-done((bf16[8,64,128]{2,1,0:T(8,128)(2,1)}, bf16[8,64,128]{2,1,0:T(8,128)(2,1)S(1)}, u32[]{:S(2)}) %copy-start) | copy-done | bytes 131096
  19.8 3.2 %tail.1 = (f32[8,64,128]{2,1,0:T(8,128)}, f32[8,8,8,128]{3,2,1,0:T(8,128)}, bf16[8,8,8,128]{3,2,1,0:T(8,128)(2,1)}) custom-call(s32[16]{0:T(128)} %vib.5, s32[1,64]{1,0:T(1,128)} %bitcast.31, s32[1,64]{1,0:T(1,128)} %bitcast.32, f32[8,64,128]{2,1,0:T(8,128)} %decode_0.1.own, bf16[8,64,128]{2,1,0:T(8,128)(2,1)} %copy-done, bf16[8,128,128]{2,1,0:T(8,128)(2,1)} %refs_1_.1, ...), custom_call_target="tpu_custom_call" | custom-call | tf_op jit(solution)/shard_map/tail/pallas_call | solution.py:178
  23.0 0.0 collective-permute-start.1
  23.0 1.6 %collective-permute-done.1 = bf16[8,8,8,128]{3,2,1,0:T(8,128)(2,1)S(1)} collective-permute-done((bf16[8,8,8,128]{3,2,1,0:T(8,128)(2,1)}, bf16[8,8,8,128]{3,2,1,0:T(8,128)(2,1)S(1)}, u32[]{:S(2)}, u32[]{:S(2)}) %collective-permute-start.1) | collective-permute-done | bytes 131104 | tf_op jit(solution)/shard_map/ppermute | solution.py:160
  24.6 1.0 %convert_add_fusion = f32[8,8,8,128]{3,2,1,0:T(8,128)S(1)} fusion(f32[8,8,8,128]{3,2,1,0:T(8,128)} %get-tuple-element.6, bf16[8,8,8,128]{3,2,1,0:T(8,128)(2,1)S(1)} %collective-permute-done.1), kind=kLoop, calls=%fused_computation | loop fusion | flops 131072 | bytes 655360 | tf_op jit(solution)/shard_map/add | solution.py:198
  25.6 2.6 %collective-permute-start.4 = (bf16[2,8,8,128]{3,2,1,0:T(8,128)(2,1)S(1)}, bf16[2,8,8,128]{3,2,1,0:T(8,128)(2,1)S(1)}, u32[]{:S(2)}, u32[]{:S(2)}) collective-permute-start(bf16[2,8,8,128]{3,2,1,0:T(8,128)(2,1)S(1)} %get-tuple-element.10), channel_id=1, source_target_pairs={{0,6},{1,7},{2,4},{3,5},{4,2},{5,3},{6,0},{7,1},{8,14},{9,15},{10,... | collective-permute-start | bytes 98312 | tf_op jit(solution)/shard_map/ppermute | solution.py:160
  28.2 0.4 %collective-permute-start.3 = (bf16[2,8,8,128]{3,2,1,0:T(8,128)(2,1)S(1)}, bf16[2,8,8,128]{3,2,1,0:T(8,128)(2,1)S(1)}, u32[]{:S(2)}, u32[]{:S(2)}) collective-permute-start(bf16[2,8,8,128]{3,2,1,0:T(8,128)(2,1)S(1)} %get-tuple-element.9), channel_id=1, source_target_pairs={{0,4},{1,5},{2,6},{3,7},{4,0},{5,1},{6,2},{7,3},{8,12},{9,13},{10,... | collective-permute-start | bytes 98312 | tf_op jit(solution)/shard_map/ppermute | solution.py:160
  28.6 0.5 %collective-permute-start.2 = (bf16[2,8,8,128]{3,2,1,0:T(8,128)(2,1)S(1)}, bf16[2,8,8,128]{3,2,1,0:T(8,128)(2,1)S(1)}, u32[]{:S(2)}, u32[]{:S(2)}) collective-permute-start(bf16[2,8,8,128]{3,2,1,0:T(8,128)(2,1)S(1)} %get-tuple-element.8), channel_id=1, source_target_pairs={{0,2},{1,3},{2,0},{3,1},{4,6},{5,7},{6,4},{7,5},{8,10},{9,11},{10,... | collective-permute-start | bytes 98312 | tf_op jit(solution)/shard_map/ppermute | solution.py:160
  29.1 1.3 %collective-permute-done.4 = bf16[2,8,8,128]{3,2,1,0:T(8,128)(2,1)S(1)} collective-permute-done((bf16[2,8,8,128]{3,2,1,0:T(8,128)(2,1)S(1)}, bf16[2,8,8,128]{3,2,1,0:T(8,128)(2,1)S(1)}, u32[]{:S(2)}, u32[]{:S(2)}) %collective-permute-start.4) | collective-permute-done | bytes 32800 | tf_op jit(solution)/shard_map/ppermute | solution.py:160
  30.5 1.6 %collective-permute-done.3 = bf16[2,8,8,128]{3,2,1,0:T(8,128)(2,1)S(1)} collective-permute-done((bf16[2,8,8,128]{3,2,1,0:T(8,128)(2,1)S(1)}, bf16[2,8,8,128]{3,2,1,0:T(8,128)(2,1)S(1)}, u32[]{:S(2)}, u32[]{:S(2)}) %collective-permute-start.3) | collective-permute-done | bytes 32800 | tf_op jit(solution)/shard_map/ppermute | solution.py:160
  32.1 0.4 %collective-permute-done.2 = bf16[2,8,8,128]{3,2,1,0:T(8,128)(2,1)S(1)} collective-permute-done((bf16[2,8,8,128]{3,2,1,0:T(8,128)(2,1)S(1)}, bf16[2,8,8,128]{3,2,1,0:T(8,128)(2,1)S(1)}, u32[]{:S(2)}, u32[]{:S(2)}) %collective-permute-start.2) | collective-permute-done | bytes 32800 | tf_op jit(solution)/shard_map/ppermute | solution.py:160
  32.6 2.7 %collective-permute-start.5 = (bf16[1,8,8,128]{3,2,1,0:T(8,128)(2,1)S(1)}, bf16[1,8,8,128]{3,2,1,0:T(8,128)(2,1)S(1)}, u32[]{:S(2)}, u32[]{:S(2)}) collective-permute-start(bf16[1,8,8,128]{3,2,1,0:T(8,128)(2,1)S(1)} %dynamic-slice_convert_fusion), channel_id=1, source_target_pairs={{0,8},{1,9},{2,10},{3,11},{4,12},{5,13},{6,14},{7,15},{8,0},{9,1},... | collective-permute-start | bytes 49160 | tf_op jit(solution)/shard_map/ppermute | solution.py:160
  35.2 2.0 %collective-permute-done.5 = bf16[1,8,8,128]{3,2,1,0:T(8,128)(2,1)S(1)} collective-permute-done((bf16[1,8,8,128]{3,2,1,0:T(8,128)(2,1)S(1)}, bf16[1,8,8,128]{3,2,1,0:T(8,128)(2,1)S(1)}, u32[]{:S(2)}, u32[]{:S(2)}) %collective-permute-start.5) | collective-permute-done | bytes 16416 | tf_op jit(solution)/shard_map/ppermute | solution.py:160
  37.3 0.6 %add_bitcast_fusion = f32[8,8,128]{2,1,0:T(8,128)} fusion(bf16[1,8,8,128]{3,2,1,0:T(8,128)(2,1)S(1)} %collective-permute-done.5, f32[2,8,8,128]{3,2,1,0:T(8,128)S(1)} %fusion.1, s32[]{:T(128)S(6)} %select_n.46), kind=kLoop, calls=%fused_computation.10 | loop fusion | flops 16384 | bytes 81924 | tf_op jit(solution)/shard_map/squeeze | solution.py:206
  (3 shorter events, 0.1 us)
Async XLA Ops:
  8.3 10.8 %collective-permute-start = (bf16[8,64,128]{2,1,0:T(8,128)(2,1)}, bf16[8,64,128]{2,1,0:T(8,128)(2,1)S(1)}, u32[]{:S(2)}, u32[]{:S(2)}) collective-permute-start(bf16[8,64,128]{2,1,0:T(8,128)(2,1)} %decode_1.1), channel_id=1, source_target_pairs={{0,16},{16,0},{1,17},{17,1},{2,18},{18,2},{3,19},{19,3},{4,20},{20... | collective-permute-start | bytes 393224 | tf_op jit(solution)/shard_map/ppermute | solution.py:173
  19.1 0.7 %copy-start = (bf16[8,64,128]{2,1,0:T(8,128)(2,1)}, bf16[8,64,128]{2,1,0:T(8,128)(2,1)S(1)}, u32[]{:S(2)}) copy-start(bf16[8,64,128]{2,1,0:T(8,128)(2,1)S(1)} %collective-permute-done.refs_0_) | copy-start | bytes 393220
  23.0 1.6 %collective-permute-start.1 = (bf16[8,8,8,128]{3,2,1,0:T(8,128)(2,1)}, bf16[8,8,8,128]{3,2,1,0:T(8,128)(2,1)S(1)}, u32[]{:S(2)}, u32[]{:S(2)}) collective-permute-start(bf16[8,8,8,128]{3,2,1,0:T(8,128)(2,1)} %get-tuple-element.7), channel_id=1, source_target_pairs={{0,1},{1,0},{2,3},{3,2},{4,5},{5,4},{6,7},{7,6},{8,9},{9,8},{10,11... | collective-permute-start | bytes 393224 | tf_op jit(solution)/shard_map/ppermute | solution.py:160
  25.6 4.9 %collective-permute-start.4 = (bf16[2,8,8,128]{3,2,1,0:T(8,128)(2,1)S(1)}, bf16[2,8,8,128]{3,2,1,0:T(8,128)(2,1)S(1)}, u32[]{:S(2)}, u32[]{:S(2)}) collective-permute-start(bf16[2,8,8,128]{3,2,1,0:T(8,128)(2,1)S(1)} %get-tuple-element.10), channel_id=1, source_target_pairs={{0,6},{1,7},{2,4},{3,5},{4,2},{5,3},{6,0},{7,1},{8,14},{9,15},{10,... | collective-permute-start | bytes 98312 | tf_op jit(solution)/shard_map/ppermute | solution.py:160
  28.2 3.9 %collective-permute-start.3 = (bf16[2,8,8,128]{3,2,1,0:T(8,128)(2,1)S(1)}, bf16[2,8,8,128]{3,2,1,0:T(8,128)(2,1)S(1)}, u32[]{:S(2)}, u32[]{:S(2)}) collective-permute-start(bf16[2,8,8,128]{3,2,1,0:T(8,128)(2,1)S(1)} %get-tuple-element.9), channel_id=1, source_target_pairs={{0,4},{1,5},{2,6},{3,7},{4,0},{5,1},{6,2},{7,3},{8,12},{9,13},{10,... | collective-permute-start | bytes 98312 | tf_op jit(solution)/shard_map/ppermute | solution.py:160
  28.6 3.9 %collective-permute-start.2 = (bf16[2,8,8,128]{3,2,1,0:T(8,128)(2,1)S(1)}, bf16[2,8,8,128]{3,2,1,0:T(8,128)(2,1)S(1)}, u32[]{:S(2)}, u32[]{:S(2)}) collective-permute-start(bf16[2,8,8,128]{3,2,1,0:T(8,128)(2,1)S(1)} %get-tuple-element.8), channel_id=1, source_target_pairs={{0,2},{1,3},{2,0},{3,1},{4,6},{5,7},{6,4},{7,5},{8,10},{9,11},{10,... | collective-permute-start | bytes 98312 | tf_op jit(solution)/shard_map/ppermute | solution.py:160
  32.6 4.7 %collective-permute-start.5 = (bf16[1,8,8,128]{3,2,1,0:T(8,128)(2,1)S(1)}, bf16[1,8,8,128]{3,2,1,0:T(8,128)(2,1)S(1)}, u32[]{:S(2)}, u32[]{:S(2)}) collective-permute-start(bf16[1,8,8,128]{3,2,1,0:T(8,128)(2,1)S(1)} %dynamic-slice_convert_fusion), channel_id=1, source_target_pairs={{0,8},{1,9},{2,10},{3,11},{4,12},{5,13},{6,14},{7,15},{8,0},{9,1},... | collective-permute-start | bytes 49160 | tf_op jit(solution)/shard_map/ppermute | solution.py:160

commit v2 on v1

--- a/solution.py
+++ b/solution.py
@@ -12,34 +12,42 @@
 F32 = jnp.float32
 SMEM = pl.BlockSpec(memory_space=pltpu.SMEM)
 VMEM = pl.BlockSpec(memory_space=pltpu.VMEM)
-ANY = pl.BlockSpec(memory_space=pl.ANY)
+HBM = pl.BlockSpec(memory_space=pltpu.HBM)
 SKEW = 16
+VMEM_LIMIT = 28 * 2**20
 
 
 def iota(shape, axis):
     return lax.broadcasted_iota(jnp.int32, shape, axis)
 
 
-def decode_kernel(vib, hadamard, pilots, records, out, held, sems, mix, pilot_rows, skewed, total, *, step, width):
+def decode_kernel(
+    vib, hadamard, pilots, records, out, held, sems, mix, backward, skewed, mixed, shifted, vib_s, signs_v, pilots_v, *, step
+):
     sweeps, channels, samples = records.shape
     owned, _, lags = out.shape
     block = mix.shape[1] // sweeps
     shift = block.bit_length() - 1
-    length = pilots.shape[1]
-    chunks = samples // width
-    groups = lax.axis_size("sweep")
+    vibrators, length = pilots.shape
+    chunks, early = sems.shape[0] - 3, shifted.shape[0]
+    width = samples // chunks
     mine = lax.axis_index("sweep")
-    group = lax.rem(mine + step, groups)
     first_sweep = mine * sweeps
-    first_code = group * owned
+    first_code = lax.rem(mine + step, lax.axis_size("sweep")) * owned
 
     def fetch(k):
-        cols = pl.ds(pl.multiple_of(k * width, width), width)
+        cols = pl.ds(k * width, width)
         return pltpu.make_async_copy(records.at[:, :, cols], held.at[:, :, cols], sems.at[k])
 
+    small = [(hadamard, signs_v), (pilots, pilots_v), (vib, vib_s)]
+    small = [pltpu.make_async_copy(x, y, sems.at[chunks + i]) for i, (x, y) in enumerate(small)]
+    for copy in small:
+        copy.start()
     for k in range(chunks):
         fetch(k).start()
-    signs = hadamard[...].astype(F32).astype(BF16)
+
+    small[0].wait()
+    signs = signs_v[...].astype(F32).astype(BF16)
     all_sweeps, codes = hadamard.shape
     rows, cols = mix.shape
     pick_code = (iota((rows, codes), 1) == first_code + (iota((rows, codes), 0) >> shift)).astype(F32).astype(BF16)
@@ -48,52 +56,74 @@
     spread = jnp.dot(by_code, pick_sweep, preferred_element_type=F32)
     same = (iota((rows, cols), 0) & (block - 1)) == (iota((rows, cols), 1) & (block - 1))
     mix[...] = jnp.where(same, spread, 0.0).astype(BF16)
-    pilot_rows[:, :length] = pilots[...].astype(F32)
-    pilot_rows[:, length:] = jnp.zeros((pilots.shape[0], samples - length), F32)
+
+    small[1].wait()
+    flip = (iota((lags, lags), 0) + iota((lags, lags), 1) == lags - 1).astype(F32).astype(BF16)
+    pieces = jnp.concatenate([pilots_v[:, j : j + lags] for j in range(0, length, lags)], axis=0)
+    pieces = jnp.dot(pieces, flip, preferred_element_type=F32)
+    for j in range(samples // lags + 1):
+        source = (samples // lags - 1 - j) * vibrators
+        inside = 0 <= source < pieces.shape[0]
+        backward[:, j * lags : (j + 1) * lags] = (
+            pieces[source : source + vibrators] if inside else jnp.zeros((vibrators, lags), F32)
+        )
+    small[2].wait()
+    made = 0
+
+    def skew(upto):
+        nonlocal made
+        while made < min(upto, owned):
+            row = backward[pl.ds(vib_s[first_code + made], 1), :]
+            wide = jnp.broadcast_to(row, (SKEW, samples + lags))
+            skewed[made] = pltpu.roll(wide, 1, 1, stride=1, stride_axis=0).astype(BF16)
+            made += 1
+
+    def shifts(c):
+        phases = [skewed[c, :, lags - j : lags - j + samples] for j in range(0, lags, SKEW)]
+        return jnp.concatenate(
+            [p[:, samples - u - lags : samples - u] for u in range(0, samples, lags) for p in phases], axis=0
+        )
+
+    skew(2)
+    for k in range(chunks):
+        fetch(k).wait()
+        for c in range(early * k // chunks, early * (k + 1) // chunks):
+            skew(c + 1)
+            shifted[c] = shifts(c)
+        skew(2 + (owned - 2) * (k + 1) // chunks)
+        for h in range(0, channels, block):
+            traces = held[:, h : h + block, k * width : (k + 1) * width].reshape(cols, width)
+            lines = jnp.dot(mix[...], traces, preferred_element_type=F32).astype(BF16)
+            for c in range(owned):
+                mixed[c, h : h + block, k * width : (k + 1) * width] = lines[c * block : (c + 1) * block]
     for c in range(owned):
-        row = pilot_rows[pl.ds(vib[first_code + c], 1), :]
-        wide = jnp.broadcast_to(row, (SKEW, samples))
-        skewed[c, :, :lags] = jnp.zeros((SKEW, lags), BF16)
-        skewed[c, :, lags:] = pltpu.roll(wide, 0, 1, stride=1, stride_axis=0).astype(BF16)
-    total[...] = jnp.zeros_like(total)
-
-    def chunk(k, carry):
-        fetch(k).wait()
-        start = pl.multiple_of(k * width, width)
-        mixed = []
-        for h in range(channels // block):
-            traces = held[:, h * block : (h + 1) * block, pl.ds(start, width)].reshape(cols, width)
-            mixed.append(jnp.dot(mix[...], traces, preferred_element_type=F32).astype(BF16))
-        for c in range(owned):
-            lines = jnp.concatenate([m[c * block : (c + 1) * block] for m in mixed], axis=0)
-            window = skewed[c, :, pl.ds(start, width + lags)]
-            shifts = [window[:, lags - j : lags - j + width] for j in range(0, lags, SKEW)]
-            total[c] += lax.dot_general(
-                lines, jnp.concatenate(shifts, axis=0), (((1,), (1,)), ((), ())), preferred_element_type=F32
-            )
-        return carry
-
-    lax.fori_loop(0, chunks, chunk, 0)
-    out[...] = total[...].astype(out.dtype)
+        kernel = shifted[c] if c < early else shifts(c)
+        out[c] = jnp.dot(mixed[c], kernel, preferred_element_type=F32).astype(out.dtype)
 
 
 def decode(vib, hadamard, pilots, records, owned, lags, step, dtype):
     sweeps, channels, samples = records.shape
     block = min(channels, 256 // sweeps)
-    width = 1024
+    chunks = 2
+    early = min(4, owned)
     return pl.pallas_call(
-        functools.partial(decode_kernel, step=step, width=width),
+        functools.partial(decode_kernel, step=step),
         out_shape=jax.ShapeDtypeStruct((owned, channels, lags), dtype),
-        in_specs=[SMEM, VMEM, VMEM, ANY],
+        in_specs=[HBM] * 4,
         out_specs=VMEM,
         scratch_shapes=[
             pltpu.VMEM((sweeps, channels, samples), BF16),
-            pltpu.SemaphoreType.DMA((samples // width,)),
+            pltpu.SemaphoreType.DMA((chunks + 3,)),
             pltpu.VMEM((owned * block, sweeps * block), BF16),
-            pltpu.VMEM((pilots.shape[0], samples), F32),
-            pltpu.VMEM((owned, SKEW, lags + samples), BF16),
-            pltpu.VMEM((owned, channels, lags), F32),
+            pltpu.VMEM((pilots.shape[0], samples + lags), F32),
+            pltpu.VMEM((owned, SKEW, samples + lags), BF16),
+            pltpu.VMEM((owned, channels, samples), BF16),
+            pltpu.VMEM((early, samples, lags), BF16),
+            pltpu.SMEM(vib.shape, jnp.int32),
+            pltpu.VMEM(hadamard.shape, jnp.int32),
+            pltpu.VMEM(pilots.shape, BF16),
         ],
+        compiler_params=pltpu.CompilerParams(vmem_limit_bytes=VMEM_LIMIT),
         cost_estimate=pl.CostEstimate(flops=8 * 10**9, bytes_accessed=records.size * 2, transcendentals=0),
         name=f"decode_{step}",
     )(vib, hadamard, pilots, records)
@@ -188,6 +218,7 @@
         in_specs=[SMEM] + [VMEM] * (5 + len(received)),
         out_specs=[VMEM] * (1 + steps[0]),
         scratch_shapes=[pltpu.VMEM((size, owned, share_rows, lags), F32)],
+        compiler_params=pltpu.CompilerParams(vmem_limit_bytes=4 * 2**20),
         name="tail",
     )(code_vibrator, owner_map.reshape(1, channels), live_mask.reshape(1, channels), own, *received, filters, targets)
     responses, held, sends = outs[0], outs[1], outs[2:]

time: 38.1 us -> 33 us (0.87)
  Pallas kernels: 18.7 us -> 10.9 us
  local copies, waits for them, and re-layouts: 0.68 us -> 4.5 us
  other arithmetic: 1.61 us -> 0.66 us
    pallas_call x2, Pallas kernels: 15.5 us -> 8.45 us  [decode(): pl.pallas_call(functools.partial(decode_kernel, step=step), out_shape=jax...]
    unnamed x2 -> x16, local copies, waits for them, and re-layouts: 0.65 us -> 4.46 us
    add x2, other arithmetic: 0.99 us -> 0.04 us  [local(): held = held + got.astype(F32)]
    pallas_call x1, Pallas kernels: 3.21 us -> 2.41 us  [local(): pl.pallas_call(functools.partial(tail_kernel, parts=len(received), radix=...]
  transfers between devices with their start and end apart: 6 -> 6, of which waited for: 5 -> 5; matrix products, arithmetic and copies ran while one was open for 0% -> 0% of each run, Pallas kernels for 20% -> 13%
where the time goes in v2:
time: 33 us; the launch traced here: 32.8 us
  Pallas kernels  10.9 us (33%)
  starting transfers between devices  9.24 us (28%)
  waiting for transfers between devices  6.81 us (21%)
  local copies, waits for them, and re-layouts  4.5 us (14%)
  between operations  0.76 us (2%)
  other arithmetic  0.66 us (2%)
    pallas_call x2, Pallas kernels, decode(): pl.pallas_call(functools.partial(decode_kernel, step=step), out_shape=jax...  8.45 us
    ppermute x5, waiting for transfers between devices, exchange(): got.append(lax.ppermute(value, 'recv', pairs))  6.8 us
    ppermute x5, starting transfers between devices, exchange(): got.append(lax.ppermute(value, 'recv', pairs))  6.21 us
    unnamed x16, local copies, waits for them, and re-layouts  4.46 us
    ppermute x1, starting transfers between devices, local(): lax.ppermute(part, 'sweep', [(i, (i + step) % groups) for i in range(grou...  3.03 us
    pallas_call x1, Pallas kernels, local(): pl.pallas_call(functools.partial(tail_kernel, parts=len(received), radix=...  2.41 us
  transfers between devices with their start and end apart: 6, of which 5 were waited for; matrix products, arithmetic and copies ran while one was open for 0% of the time, Pallas kernels for 13%

profile of v2, /device:TPU:0, one launch (start us, length us, event | category | flops | bytes accessed | tf_op | source)
XLA Modules:
  0.0 32.8 jit_solution(4680782868567121825)
XLA Ops:
  0.6 0.0 copy-start.2
  0.6 0.6 %copy-done.2 = s32[16]{0:T(128)S(1)} copy-done((s32[16]{0:T(128)S(1)}, s32[16]{0:T(128)}, u32[]{:S(2)}) %copy-start.2) | copy-done | bytes 88
  1.3 0.0 copy-start.5
  1.3 2.2 %copy-done.5 = bf16[8,64,4096]{2,1,0:T(8,128)(2,1)S(1)} copy-done((bf16[8,64,4096]{2,1,0:T(8,128)(2,1)S(1)}, bf16[8,64,4096]{2,1,0:T(8,128)(2,1)}, u32[]{:S(2)}) %copy-start.5) | copy-done | bytes 4194328
  3.5 0.0 copy-start.6
  3.5 0.9 %copy-done.6 = bf16[16,3968]{1,0:T(8,128)(2,1)S(1)} copy-done((bf16[16,3968]{1,0:T(8,128)(2,1)S(1)}, bf16[16,3968]{1,0:T(8,128)(2,1)}, u32[]{:S(2)}) %copy-start.6) | copy-done | bytes 127000
  4.4 0.0 copy-start.7
  4.4 0.7 %copy-done.7 = s32[16,16]{1,0:T(8,128)S(1)} copy-done((s32[16,16]{1,0:T(8,128)S(1)}, s32[16,16]{1,0:T(8,128)}, u32[]{:S(2)}) %copy-start.7) | copy-done | bytes 1048
  5.1 4.2 %decode_1.1 = bf16[8,64,128]{2,1,0:T(8,128)(2,1)S(1)} custom-call(s32[16]{0:T(128)S(1)} %copy-done.2, s32[16,16]{1,0:T(8,128)S(1)} %copy-done.7, bf16[16,3968]{1,0:T(8,128)(2,1)S(1)} %copy-done.6, bf16[8,64,4096]{2,1,0:T(8,128)(2,1)S(1)} %copy-done.5), custom_call_target="tpu_custom_call" | custom-call | flops 8000000000 | bytes 4194304 | tf_op jit(solution)/shard_map/decode_1/pallas_call | solution.py:109
  9.3 0.0 copy-start
  9.3 0.0 copy-start.1
  9.3 0.0 copy-start.3
  9.3 0.0 copy-start.4
  9.4 3.0 %collective-permute-start = (bf16[8,64,128]{2,1,0:T(8,128)(2,1)S(1)}, bf16[8,64,128]{2,1,0:T(8,128)(2,1)S(1)}, u32[]{:S(2)}, u32[]{:S(2)}) collective-permute-start(bf16[8,64,128]{2,1,0:T(8,128)(2,1)S(1)} %decode_1.1), channel_id=1, source_target_pairs={{0,16},{16,0},{1,17},{17,1},{2,18},{18,2},{3,19},{19,3},{4,20},{20... | collective-permute-start | bytes 393224 | tf_op jit(solution)/shard_map/ppermute | solution.py:203
  12.4 4.2 %decode_0.1.own = f32[8,64,128]{2,1,0:T(8,128)S(1)} custom-call(s32[16]{0:T(128)S(1)} %copy-done.2, s32[16,16]{1,0:T(8,128)S(1)} %copy-done.7, bf16[16,3968]{1,0:T(8,128)(2,1)S(1)} %copy-done.6, bf16[8,64,4096]{2,1,0:T(8,128)(2,1)S(1)} %copy-done.5), custom_call_target="tpu_custom_call" | custom-call | flops 8000000000 | bytes 4194304 | tf_op jit(solution)/shard_map/decode_0/pallas_call | solution.py:109
  16.6 0.0 collective-permute-done.refs_0_
  16.6 0.0 copy-done
  16.6 0.0 copy-done.1
  16.7 0.0 copy-done.3
  16.7 0.0 copy-done.4
  16.7 2.4 %tail.1 = (f32[8,64,128]{2,1,0:T(8,128)}, f32[8,8,8,128]{3,2,1,0:T(8,128)S(1)}, bf16[8,8,8,128]{3,2,1,0:T(8,128)(2,1)S(1)}) custom-call(s32[16]{0:T(128)S(1)} %copy-done.2, s32[1,64]{1,0:T(1,128)S(1)} %bitcast.29, s32[1,64]{1,0:T(1,128)S(1)} %bitcast.30, f32[8,64,128]{2,1,0:T(8,128)S(1)} %decode_0.1.own, ...), custom_call_target="tpu_custom_call" | custom-call | tf_op jit(solution)/shard_map/tail/pallas_call | solution.py:208
  19.1 0.0 collective-permute-start.1
  19.1 1.3 %collective-permute-done.1 = bf16[8,8,8,128]{3,2,1,0:T(8,128)(2,1)S(1)} collective-permute-done((bf16[8,8,8,128]{3,2,1,0:T(8,128)(2,1)S(1)}, bf16[8,8,8,128]{3,2,1,0:T(8,128)(2,1)S(1)}, u32[]{:S(2)}, u32[]{:S(2)}) %collective-permute-start.1) | collective-permute-done | bytes 131104 | tf_op jit(solution)/shard_map/ppermute | solution.py:190
  20.5 2.6 %collective-permute-start.4 = (bf16[2,8,8,128]{3,2,1,0:T(8,128)(2,1)S(1)}, bf16[2,8,8,128]{3,2,1,0:T(8,128)(2,1)S(1)}, u32[]{:S(2)}, u32[]{:S(2)}) collective-permute-start(bf16[2,8,8,128]{3,2,1,0:T(8,128)(2,1)S(1)} %get-tuple-element.10), channel_id=1, source_target_pairs={{0,6},{1,7},{2,4},{3,5},{4,2},{5,3},{6,0},{7,1},{8,14},{9,15},{10,... | collective-permute-start | bytes 98312 | tf_op jit(solution)/shard_map/ppermute | solution.py:190
  23.1 0.4 %collective-permute-start.3 = (bf16[2,8,8,128]{3,2,1,0:T(8,128)(2,1)S(1)}, bf16[2,8,8,128]{3,2,1,0:T(8,128)(2,1)S(1)}, u32[]{:S(2)}, u32[]{:S(2)}) collective-permute-start(bf16[2,8,8,128]{3,2,1,0:T(8,128)(2,1)S(1)} %get-tuple-element.9), channel_id=1, source_target_pairs={{0,4},{1,5},{2,6},{3,7},{4,0},{5,1},{6,2},{7,3},{8,12},{9,13},{10,... | collective-permute-start | bytes 98312 | tf_op jit(solution)/shard_map/ppermute | solution.py:190
  23.5 0.5 %collective-permute-start.2 = (bf16[2,8,8,128]{3,2,1,0:T(8,128)(2,1)S(1)}, bf16[2,8,8,128]{3,2,1,0:T(8,128)(2,1)S(1)}, u32[]{:S(2)}, u32[]{:S(2)}) collective-permute-start(bf16[2,8,8,128]{3,2,1,0:T(8,128)(2,1)S(1)} %get-tuple-element.8), channel_id=1, source_target_pairs={{0,2},{1,3},{2,0},{3,1},{4,6},{5,7},{6,4},{7,5},{8,10},{9,11},{10,... | collective-permute-start | bytes 98312 | tf_op jit(solution)/shard_map/ppermute | solution.py:190
  24.1 1.3 %collective-permute-done.4 = bf16[2,8,8,128]{3,2,1,0:T(8,128)(2,1)S(1)} collective-permute-done((bf16[2,8,8,128]{3,2,1,0:T(8,128)(2,1)S(1)}, bf16[2,8,8,128]{3,2,1,0:T(8,128)(2,1)S(1)}, u32[]{:S(2)}, u32[]{:S(2)}) %collective-permute-start.4) | collective-permute-done | bytes 32800 | tf_op jit(solution)/shard_map/ppermute | solution.py:190
  25.4 1.6 %collective-permute-done.3 = bf16[2,8,8,128]{3,2,1,0:T(8,128)(2,1)S(1)} collective-permute-done((bf16[2,8,8,128]{3,2,1,0:T(8,128)(2,1)S(1)}, bf16[2,8,8,128]{3,2,1,0:T(8,128)(2,1)S(1)}, u32[]{:S(2)}, u32[]{:S(2)}) %collective-permute-start.3) | collective-permute-done | bytes 32800 | tf_op jit(solution)/shard_map/ppermute | solution.py:190
  27.0 0.4 %collective-permute-done.2 = bf16[2,8,8,128]{3,2,1,0:T(8,128)(2,1)S(1)} collective-permute-done((bf16[2,8,8,128]{3,2,1,0:T(8,128)(2,1)S(1)}, bf16[2,8,8,128]{3,2,1,0:T(8,128)(2,1)S(1)}, u32[]{:S(2)}, u32[]{:S(2)}) %collective-permute-start.2) | collective-permute-done | bytes 32800 | tf_op jit(solution)/shard_map/ppermute | solution.py:190
  27.5 2.7 %collective-permute-start.5 = (bf16[1,8,8,128]{3,2,1,0:T(8,128)(2,1)S(1)}, bf16[1,8,8,128]{3,2,1,0:T(8,128)(2,1)S(1)}, u32[]{:S(2)}, u32[]{:S(2)}) collective-permute-start(bf16[1,8,8,128]{3,2,1,0:T(8,128)(2,1)S(1)} %dynamic-slice_convert_fusion), channel_id=1, source_target_pairs={{0,8},{1,9},{2,10},{3,11},{4,12},{5,13},{6,14},{7,15},{8,0},{9,1},... | collective-permute-start | bytes 49160 | tf_op jit(solution)/shard_map/ppermute | solution.py:190
  30.2 2.1 %collective-permute-done.5 = bf16[1,8,8,128]{3,2,1,0:T(8,128)(2,1)S(1)} collective-permute-done((bf16[1,8,8,128]{3,2,1,0:T(8,128)(2,1)S(1)}, bf16[1,8,8,128]{3,2,1,0:T(8,128)(2,1)S(1)}, u32[]{:S(2)}, u32[]{:S(2)}) %collective-permute-start.5) | collective-permute-done | bytes 16416 | tf_op jit(solution)/shard_map/ppermute | solution.py:190
  32.2 0.6 %add_bitcast_fusion = f32[8,8,128]{2,1,0:T(8,128)} fusion(bf16[1,8,8,128]{3,2,1,0:T(8,128)(2,1)S(1)} %collective-permute-done.5, f32[2,8,8,128]{3,2,1,0:T(8,128)S(1)} %fusion.1, s32[]{:T(128)S(6)} %select_n.46), kind=kLoop, calls=%fused_computation.10 | loop fusion | flops 16384 | bytes 81924 | tf_op jit(solution)/shard_map/squeeze | solution.py:237
  (4 shorter events, 0.1 us)
Async XLA Ops:
  0.6 0.7 %copy-start.2 = (s32[16]{0:T(128)S(1)}, s32[16]{0:T(128)}, u32[]{:S(2)}) copy-start(s32[16]{0:T(128)} %vib.5) | copy-start | bytes 196
  1.3 2.2 %copy-start.5 = (bf16[8,64,4096]{2,1,0:T(8,128)(2,1)S(1)}, bf16[8,64,4096]{2,1,0:T(8,128)(2,1)}, u32[]{:S(2)}) copy-start(bf16[8,64,4096]{2,1,0:T(8,128)(2,1)} %records.3) | copy-start | bytes 12582916
  3.5 0.9 %copy-start.6 = (bf16[16,3968]{1,0:T(8,128)(2,1)S(1)}, bf16[16,3968]{1,0:T(8,128)(2,1)}, u32[]{:S(2)}) copy-start(bf16[16,3968]{1,0:T(8,128)(2,1)} %pilots.3) | copy-start | bytes 380932
  4.4 0.7 %copy-start.7 = (s32[16,16]{1,0:T(8,128)S(1)}, s32[16,16]{1,0:T(8,128)}, u32[]{:S(2)}) copy-start(s32[16,16]{1,0:T(8,128)} %hadamard.3) | copy-start | bytes 3076
  9.3 7.3 %copy-start = (bf16[8,128,128]{2,1,0:T(8,128)(2,1)S(1)}, bf16[8,128,128]{2,1,0:T(8,128)(2,1)}, u32[]{:S(2)}) copy-start(bf16[8,128,128]{2,1,0:T(8,128)(2,1)} %refs_1_.1) | copy-start | bytes 786436
  9.3 7.3 %copy-start.1 = (bf16[8,64,128]{2,1,0:T(8,128)(2,1)S(1)}, bf16[8,64,128]{2,1,0:T(8,128)(2,1)}, u32[]{:S(2)}) copy-start(bf16[8,64,128]{2,1,0:T(8,128)(2,1)} %refs_2_.1) | copy-start | bytes 393220
  9.3 7.3 %copy-start.3 = (s32[64]{0:T(128)S(1)}, s32[64]{0:T(128)}, u32[]{:S(2)}) copy-start(s32[64]{0:T(128)} %param.12) | copy-start | bytes 772
  9.3 7.3 %copy-start.4 = (s32[64]{0:T(128)S(1)}, s32[64]{0:T(128)}, u32[]{:S(2)}) copy-start(s32[64]{0:T(128)} %param.13) | copy-start | bytes 772
  9.4 7.3 %collective-permute-start = (bf16[8,64,128]{2,1,0:T(8,128)(2,1)S(1)}, bf16[8,64,128]{2,1,0:T(8,128)(2,1)S(1)}, u32[]{:S(2)}, u32[]{:S(2)}) collective-permute-start(bf16[8,64,128]{2,1,0:T(8,128)(2,1)S(1)} %decode_1.1), channel_id=1, source_target_pairs={{0,16},{16,0},{1,17},{17,1},{2,18},{18,2},{3,19},{19,3},{4,20},{20... | collective-permute-start | bytes 393224 | tf_op jit(solution)/shard_map/ppermute | solution.py:203
  19.1 1.3 %collective-permute-start.1 = (bf16[8,8,8,128]{3,2,1,0:T(8,128)(2,1)S(1)}, bf16[8,8,8,128]{3,2,1,0:T(8,128)(2,1)S(1)}, u32[]{:S(2)}, u32[]{:S(2)}) collective-permute-start(bf16[8,8,8,128]{3,2,1,0:T(8,128)(2,1)S(1)} %get-tuple-element.7), channel_id=1, source_target_pairs={{0,1},{1,0},{2,3},{3,2},{4,5},{5,4},{6,7},{7,6},{8,9},{9,8},{10,11... | collective-permute-start | bytes 393224 | tf_op jit(solution)/shard_map/ppermute | solution.py:190
  20.5 4.9 %collective-permute-start.4 = (bf16[2,8,8,128]{3,2,1,0:T(8,128)(2,1)S(1)}, bf16[2,8,8,128]{3,2,1,0:T(8,128)(2,1)S(1)}, u32[]{:S(2)}, u32[]{:S(2)}) collective-permute-start(bf16[2,8,8,128]{3,2,1,0:T(8,128)(2,1)S(1)} %get-tuple-element.10), channel_id=1, source_target_pairs={{0,6},{1,7},{2,4},{3,5},{4,2},{5,3},{6,0},{7,1},{8,14},{9,15},{10,... | collective-permute-start | bytes 98312 | tf_op jit(solution)/shard_map/ppermute | solution.py:190
  23.1 3.9 %collective-permute-start.3 = (bf16[2,8,8,128]{3,2,1,0:T(8,128)(2,1)S(1)}, bf16[2,8,8,128]{3,2,1,0:T(8,128)(2,1)S(1)}, u32[]{:S(2)}, u32[]{:S(2)}) collective-permute-start(bf16[2,8,8,128]{3,2,1,0:T(8,128)(2,1)S(1)} %get-tuple-element.9), channel_id=1, source_target_pairs={{0,4},{1,5},{2,6},{3,7},{4,0},{5,1},{6,2},{7,3},{8,12},{9,13},{10,... | collective-permute-start | bytes 98312 | tf_op jit(solution)/shard_map/ppermute | solution.py:190
  23.5 3.9 %collective-permute-start.2 = (bf16[2,8,8,128]{3,2,1,0:T(8,128)(2,1)S(1)}, bf16[2,8,8,128]{3,2,1,0:T(8,128)(2,1)S(1)}, u32[]{:S(2)}, u32[]{:S(2)}) collective-permute-start(bf16[2,8,8,128]{3,2,1,0:T(8,128)(2,1)S(1)} %get-tuple-element.8), channel_id=1, source_target_pairs={{0,2},{1,3},{2,0},{3,1},{4,6},{5,7},{6,4},{7,5},{8,10},{9,11},{10,... | collective-permute-start | bytes 98312 | tf_op jit(solution)/shard_map/ppermute | solution.py:190
  27.5 4.7 %collective-permute-start.5 = (bf16[1,8,8,128]{3,2,1,0:T(8,128)(2,1)S(1)}, bf16[1,8,8,128]{3,2,1,0:T(8,128)(2,1)S(1)}, u32[]{:S(2)}, u32[]{:S(2)}) collective-permute-start(bf16[1,8,8,128]{3,2,1,0:T(8,128)(2,1)S(1)} %dynamic-slice_convert_fusion), channel_id=1, source_target_pairs={{0,8},{1,9},{2,10},{3,11},{4,12},{5,13},{6,14},{7,15},{8,0},{9,1},... | collective-permute-start | bytes 49160 | tf_op jit(solution)/shard_map/ppermute | solution.py:190

commit v3 on v2

--- a/solution.py
+++ b/solution.py
@@ -14,6 +14,7 @@
 VMEM = pl.BlockSpec(memory_space=pltpu.VMEM)
 HBM = pl.BlockSpec(memory_space=pltpu.HBM)
 SKEW = 16
+CHUNKS = 2
 VMEM_LIMIT = 28 * 2**20
 
 
@@ -21,16 +22,18 @@
     return lax.broadcasted_iota(jnp.int32, shape, axis)
 
 
-def decode_kernel(
-    vib, hadamard, pilots, records, out, held, sems, mix, backward, skewed, mixed, shifted, vib_s, signs_v, pilots_v, *, step
-):
-    sweeps, channels, samples = records.shape
+def decode_kernel(*refs, step, first):
+    if first:
+        vib, hadamard, pilots, records, out, held, signs_v, ordered, mix, skewed, mixed, shifted, sems, vib_s, pilots_v, backward = refs
+    else:
+        held, signs_v, ordered, out, mix, skewed, mixed, shifted = refs
+    sweeps, channels, samples = held.shape
     owned, _, lags = out.shape
+    all_sweeps, codes = signs_v.shape
     block = mix.shape[1] // sweeps
     shift = block.bit_length() - 1
-    vibrators, length = pilots.shape
-    chunks, early = sems.shape[0] - 3, shifted.shape[0]
-    width = samples // chunks
+    early = shifted.shape[0]
+    width = samples // CHUNKS
     mine = lax.axis_index("sweep")
     first_sweep = mine * sweeps
     first_code = lax.rem(mine + step, lax.axis_size("sweep")) * owned
@@ -39,16 +42,16 @@
         cols = pl.ds(k * width, width)
         return pltpu.make_async_copy(records.at[:, :, cols], held.at[:, :, cols], sems.at[k])
 
-    small = [(hadamard, signs_v), (pilots, pilots_v), (vib, vib_s)]
-    small = [pltpu.make_async_copy(x, y, sems.at[chunks + i]) for i, (x, y) in enumerate(small)]
-    for copy in small:
-        copy.start()
-    for k in range(chunks):
-        fetch(k).start()
-
-    small[0].wait()
+    if first:
+        small = [(hadamard, signs_v), (pilots, pilots_v), (vib, vib_s)]
+        small = [pltpu.make_async_copy(x, y, sems.at[CHUNKS + i]) for i, (x, y) in enumerate(small)]
+        for copy in small:
+            copy.start()
+        for k in range(CHUNKS):
+            fetch(k).start()
+        small[0].wait()
+
     signs = signs_v[...].astype(F32).astype(BF16)
-    all_sweeps, codes = hadamard.shape
     rows, cols = mix.shape
     pick_code = (iota((rows, codes), 1) == first_code + (iota((rows, codes), 0) >> shift)).astype(F32).astype(BF16)
     pick_sweep = (iota((all_sweeps, cols), 0) == first_sweep + (iota((all_sweeps, cols), 1) >> shift)).astype(F32).astype(BF16)
@@ -57,23 +60,27 @@
     same = (iota((rows, cols), 0) & (block - 1)) == (iota((rows, cols), 1) & (block - 1))
     mix[...] = jnp.where(same, spread, 0.0).astype(BF16)
 
-    small[1].wait()
-    flip = (iota((lags, lags), 0) + iota((lags, lags), 1) == lags - 1).astype(F32).astype(BF16)
-    pieces = jnp.concatenate([pilots_v[:, j : j + lags] for j in range(0, length, lags)], axis=0)
-    pieces = jnp.dot(pieces, flip, preferred_element_type=F32)
-    for j in range(samples // lags + 1):
-        source = (samples // lags - 1 - j) * vibrators
-        inside = 0 <= source < pieces.shape[0]
-        backward[:, j * lags : (j + 1) * lags] = (
-            pieces[source : source + vibrators] if inside else jnp.zeros((vibrators, lags), F32)
-        )
-    small[2].wait()
+    if first:
+        small[1].wait()
+        vibrators, length = pilots.shape
+        flip = (iota((lags, lags), 0) + iota((lags, lags), 1) == lags - 1).astype(F32).astype(BF16)
+        pieces = jnp.concatenate([pilots_v[:, j : j + lags] for j in range(0, length, lags)], axis=0)
+        pieces = jnp.dot(pieces, flip, preferred_element_type=F32)
+        for j in range(samples // lags + 1):
+            source = (samples // lags - 1 - j) * vibrators
+            inside = 0 <= source < pieces.shape[0]
+            backward[:, j * lags : (j + 1) * lags] = (
+                pieces[source : source + vibrators] if inside else jnp.zeros((vibrators, lags), F32)
+            )
+        small[2].wait()
+        for c in range(codes):
+            ordered[pl.ds(c, 1), :] = backward[pl.ds(vib_s[c], 1), :]
     made = 0
 
     def skew(upto):
         nonlocal made
         while made < min(upto, owned):
-            row = backward[pl.ds(vib_s[first_code + made], 1), :]
+            row = ordered[pl.ds(first_code + made, 1), :]
             wide = jnp.broadcast_to(row, (SKEW, samples + lags))
             skewed[made] = pltpu.roll(wide, 1, 1, stride=1, stride_axis=0).astype(BF16)
             made += 1
@@ -85,12 +92,13 @@
         )
 
     skew(2)
-    for k in range(chunks):
-        fetch(k).wait()
-        for c in range(early * k // chunks, early * (k + 1) // chunks):
+    for k in range(CHUNKS):
+        if first:
+            fetch(k).wait()
+        for c in range(early * k // CHUNKS, early * (k + 1) // CHUNKS):
             skew(c + 1)
             shifted[c] = shifts(c)
-        skew(2 + (owned - 2) * (k + 1) // chunks)
+        skew(2 + (owned - 2) * (k + 1) // CHUNKS)
         for h in range(0, channels, block):
             traces = held[:, h : h + block, k * width : (k + 1) * width].reshape(cols, width)
             lines = jnp.dot(mix[...], traces, preferred_element_type=F32).astype(BF16)
@@ -101,32 +109,41 @@
         out[c] = jnp.dot(mixed[c], kernel, preferred_element_type=F32).astype(out.dtype)
 
 
-def decode(vib, hadamard, pilots, records, owned, lags, step, dtype):
-    sweeps, channels, samples = records.shape
+def decode(inputs, shape, owned, codes, lags, step, dtype, first):
+    sweeps, channels, samples = shape
     block = min(channels, 256 // sweeps)
-    chunks = 2
     early = min(4, owned)
+    out_shape = [pltpu.VMEM((owned, channels, lags), dtype)]
+    scratch = [
+        pltpu.VMEM((owned * block, sweeps * block), BF16),
+        pltpu.VMEM((owned, SKEW, samples + lags), BF16),
+        pltpu.VMEM((owned, channels, samples), BF16),
+        pltpu.VMEM((early, samples, lags), BF16),
+    ]
+    if first:
+        vib, hadamard, pilots, _ = inputs
+        inputs = [pltpu.with_memory_space_constraint(x, pltpu.HBM) for x in inputs]
+        out_shape += [
+            pltpu.VMEM(shape, BF16),
+            pltpu.VMEM(hadamard.shape, jnp.int32),
+            pltpu.VMEM((codes, samples + lags), F32),
+        ]
+        scratch += [
+            pltpu.SemaphoreType.DMA((CHUNKS + 3,)),
+            pltpu.SMEM(vib.shape, jnp.int32),
+            pltpu.VMEM(pilots.shape, BF16),
+            pltpu.VMEM((pilots.shape[0], samples + lags), F32),
+        ]
     return pl.pallas_call(
-        functools.partial(decode_kernel, step=step),
-        out_shape=jax.ShapeDtypeStruct((owned, channels, lags), dtype),
-        in_specs=[HBM] * 4,
-        out_specs=VMEM,
-        scratch_shapes=[
-            pltpu.VMEM((sweeps, channels, samples), BF16),
-            pltpu.SemaphoreType.DMA((chunks + 3,)),
-            pltpu.VMEM((owned * block, sweeps * block), BF16),
-            pltpu.VMEM((pilots.shape[0], samples + lags), F32),
-            pltpu.VMEM((owned, SKEW, samples + lags), BF16),
-            pltpu.VMEM((owned, channels, samples), BF16),
-            pltpu.VMEM((early, samples, lags), BF16),
-            pltpu.SMEM(vib.shape, jnp.int32),
-            pltpu.VMEM(hadamard.shape, jnp.int32),
-            pltpu.VMEM(pilots.shape, BF16),
-        ],
+        functools.partial(decode_kernel, step=step, first=first),
+        out_shape=out_shape,
+        in_specs=[HBM if first else VMEM] * len(inputs),
+        out_specs=[VMEM] * len(out_shape),
+        scratch_shapes=scratch,
         compiler_params=pltpu.CompilerParams(vmem_limit_bytes=VMEM_LIMIT),
-        cost_estimate=pl.CostEstimate(flops=8 * 10**9, bytes_accessed=records.size * 2, transcendentals=0),
+        cost_estimate=pl.CostEstimate(flops=8 * 10**9, bytes_accessed=math.prod(shape) * 2, transcendentals=0),
         name=f"decode_{step}",
-    )(vib, hadamard, pilots, records)
+    )(*inputs)
 
 
 def tail_kernel(vib, owner, live, own, *refs, parts, radix, norm, factor):
@@ -198,10 +215,15 @@
     owned, lags, _ = filters.shape
     channels = records.shape[1]
     received = []
-    for step in range(1, groups):
-        part = decode(code_vibrator, hadamard, pilots, records, owned, lags, step, BF16)
-        received.append(lax.ppermute(part, "sweep", [(i, (i + step) % groups) for i in range(groups)]))
-    own = decode(code_vibrator, hadamard, pilots, records, owned, lags, 0, F32)
+    inputs = (code_vibrator, hadamard, pilots, records)
+    for step in list(range(1, groups)) + [0]:
+        dtype = BF16 if step else F32
+        part, *extra = decode(inputs, records.shape, owned, codes, lags, step, dtype, len(inputs) == 4)
+        if extra:
+            inputs = tuple(extra)
+        if step:
+            received.append(lax.ppermute(part, "sweep", [(i, (i + step) % groups) for i in range(groups)]))
+    own = part
     steps = radices(size)
     share_rows = lags // size
     piece = (size // steps[0], owned, share_rows, lags)

time: 33 us -> 28.3 us (0.86)
  local copies, waits for them, and re-layouts: 4.5 us -> 0.06 us
  Pallas kernels: 10.9 us -> 9.76 us
  waiting for transfers between devices: 6.81 us -> 7.67 us
    unnamed x16 -> x10, local copies, waits for them, and re-layouts: 4.46 us -> 0.02 us
    pallas_call x2, Pallas kernels: 8.45 us -> 7.36 us  [decode(): pl.pallas_call(functools.partial(decode_kernel, step=step, first=first),...]
    ppermute x1, waiting for transfers between devices: 0.01 us -> 0.62 us  [local(): lax.ppermute(part, 'sweep', [(i, (i + step) % groups) for i in range(grou...]
  transfers between devices with their start and end apart: 6 -> 6, of which waited for: 5 -> 6; matrix products, arithmetic and copies ran while one was open for 0% -> 0% of each run, Pallas kernels for 13% -> 10%
where the time goes in v3:
time: 28.3 us; the launch traced here: 28.1 us
  Pallas kernels  9.76 us (34%)
  starting transfers between devices  9.23 us (33%)
  waiting for transfers between devices  7.67 us (27%)
  between operations  0.71 us (3%)
  other arithmetic  0.66 us (2%)
    pallas_call x2, Pallas kernels, decode(): pl.pallas_call(functools.partial(decode_kernel, step=step, first=first),...  7.36 us
    ppermute x5, waiting for transfers between devices, exchange(): got.append(lax.ppermute(value, 'recv', pairs))  7.05 us
    ppermute x5, starting transfers between devices, exchange(): got.append(lax.ppermute(value, 'recv', pairs))  6.21 us
    ppermute x1, starting transfers between devices, local(): lax.ppermute(part, 'sweep', [(i, (i + step) % groups) for i in range(grou...  3.03 us
    pallas_call x1, Pallas kernels, local(): pl.pallas_call(functools.partial(tail_kernel, parts=len(received), radix=...  2.41 us
    ppermute x1, waiting for transfers between devices, local(): lax.ppermute(part, 'sweep', [(i, (i + step) % groups) for i in range(grou...  0.62 us
    squeeze x1, other arithmetic, local(): return (responses, held[0])  0.62 us
  transfers between devices with their start and end apart: 6, of which 6 were waited for; matrix products, arithmetic and copies ran while one was open for 0% of the time, Pallas kernels for 10%

profile of v3, /device:TPU:0, one launch (start us, length us, event | category | flops | bytes accessed | tf_op | source)
XLA Modules:
  0.0 28.1 jit_solution(7546961858250430550)
XLA Ops:
  0.6 4.5 %decode_1.1 = (bf16[8,64,128]{2,1,0:T(8,128)(2,1)S(1)}, bf16[8,64,4096]{2,1,0:T(8,128)(2,1)S(1)}, s32[16,16]{1,0:T(8,128)S(1)}, f32[16,4224]{1,0:T(8,128)S(1)}) custom-call(s32[16]{0:T(128)} %vib.1, s32[16,16]{1,0:T(8,128)} %refs_1_.2, bf16[16,3968]{1,0:T(8,128)(2,1)} %refs_2_.2, bf16[8,64,4096]{2,1,0:T(8,128)(2,1)} %refs_3_.1), custom_call_target="tpu_custom_call" | custom-call | flops 8000000000 | bytes 4194304 | tf_op jit(solution)/shard_map/decode_1/pallas_call | solution.py:137
  5.1 3.0 %collective-permute-start = (bf16[8,64,128]{2,1,0:T(8,128)(2,1)S(1)}, bf16[8,64,128]{2,1,0:T(8,128)(2,1)S(1)}, u32[]{:S(2)}, u32[]{:S(2)}) collective-permute-start(bf16[8,64,128]{2,1,0:T(8,128)(2,1)S(1)} %get-tuple-element.12), channel_id=1, source_target_pairs={{0,16},{16,0},{1,17},{17,1},{2,18},{18,2},{3,19},{19,3},{4,20},{20... | collective-permute-start | bytes 393224 | tf_op jit(solution)/shard_map/ppermute | solution.py:225
  8.2 0.0 copy-start
  8.2 0.0 copy-start.1
  8.2 0.0 copy-start.2
  8.2 0.0 copy-start.3
  8.2 0.0 copy-start.4
  8.2 2.8 %decode_0.1.own = f32[8,64,128]{2,1,0:T(8,128)S(1)} custom-call(bf16[8,64,4096]{2,1,0:T(8,128)(2,1)S(1)} %get-tuple-element.9.refs_0_, s32[16,16]{1,0:T(8,128)S(1)} %get-tuple-element.10.refs_1_, f32[16,4224]{1,0:T(8,128)S(1)} %get-tuple-element.11.refs_2_), custom_call_target="tpu_custom_call" | custom-call | flops 8000000000 | bytes 4194304 | tf_op jit(solution)/shard_map/decode_0/pallas_call | solution.py:137
  11.0 0.6 %collective-permute-done.refs_0_ = bf16[8,64,128]{2,1,0:T(8,128)(2,1)S(1)} collective-permute-done((bf16[8,64,128]{2,1,0:T(8,128)(2,1)S(1)}, bf16[8,64,128]{2,1,0:T(8,128)(2,1)S(1)}, u32[]{:S(2)}, u32[]{:S(2)}) %collective-permute-start) | collective-permute-done | bytes 131104 | tf_op jit(solution)/shard_map/ppermute | solution.py:225
  11.7 0.0 copy-done
  11.7 0.0 copy-done.1
  11.7 0.0 copy-done.2
  11.7 0.0 copy-done.3
  11.7 0.0 copy-done.4
  11.7 2.4 %tail.1 = (f32[8,64,128]{2,1,0:T(8,128)}, f32[8,8,8,128]{3,2,1,0:T(8,128)S(1)}, bf16[8,8,8,128]{3,2,1,0:T(8,128)(2,1)S(1)}) custom-call(s32[16]{0:T(128)S(1)} %copy-done.2, s32[1,64]{1,0:T(1,128)S(1)} %bitcast.29, s32[1,64]{1,0:T(1,128)S(1)} %bitcast.30, f32[8,64,128]{2,1,0:T(8,128)S(1)} %decode_0.1.own, ...), custom_call_target="tpu_custom_call" | custom-call | tf_op jit(solution)/shard_map/tail/pallas_call | solution.py:230
  14.1 0.0 collective-permute-start.1
  14.1 1.3 %collective-permute-done.1 = bf16[8,8,8,128]{3,2,1,0:T(8,128)(2,1)S(1)} collective-permute-done((bf16[8,8,8,128]{3,2,1,0:T(8,128)(2,1)S(1)}, bf16[8,8,8,128]{3,2,1,0:T(8,128)(2,1)S(1)}, u32[]{:S(2)}, u32[]{:S(2)}) %collective-permute-start.1) | collective-permute-done | bytes 131104 | tf_op jit(solution)/shard_map/ppermute | solution.py:207
  15.5 2.8 %collective-permute-start.4 = (bf16[2,8,8,128]{3,2,1,0:T(8,128)(2,1)S(1)}, bf16[2,8,8,128]{3,2,1,0:T(8,128)(2,1)S(1)}, u32[]{:S(2)}, u32[]{:S(2)}) collective-permute-start(bf16[2,8,8,128]{3,2,1,0:T(8,128)(2,1)S(1)} %get-tuple-element.18), channel_id=1, source_target_pairs={{0,6},{1,7},{2,4},{3,5},{4,2},{5,3},{6,0},{7,1},{8,14},{9,15},{10,... | collective-permute-start | bytes 98312 | tf_op jit(solution)/shard_map/ppermute | solution.py:207
  18.4 0.4 %collective-permute-start.3 = (bf16[2,8,8,128]{3,2,1,0:T(8,128)(2,1)S(1)}, bf16[2,8,8,128]{3,2,1,0:T(8,128)(2,1)S(1)}, u32[]{:S(2)}, u32[]{:S(2)}) collective-permute-start(bf16[2,8,8,128]{3,2,1,0:T(8,128)(2,1)S(1)} %get-tuple-element.17), channel_id=1, source_target_pairs={{0,4},{1,5},{2,6},{3,7},{4,0},{5,1},{6,2},{7,3},{8,12},{9,13},{10,... | collective-permute-start | bytes 98312 | tf_op jit(solution)/shard_map/ppermute | solution.py:207
  18.8 0.3 collective-permute-start.2
  19.1 1.3 %collective-permute-done.4 = bf16[2,8,8,128]{3,2,1,0:T(8,128)(2,1)S(1)} collective-permute-done((bf16[2,8,8,128]{3,2,1,0:T(8,128)(2,1)S(1)}, bf16[2,8,8,128]{3,2,1,0:T(8,128)(2,1)S(1)}, u32[]{:S(2)}, u32[]{:S(2)}) %collective-permute-start.4) | collective-permute-done | bytes 32800 | tf_op jit(solution)/shard_map/ppermute | solution.py:207
  20.4 1.9 %collective-permute-done.3 = bf16[2,8,8,128]{3,2,1,0:T(8,128)(2,1)S(1)} collective-permute-done((bf16[2,8,8,128]{3,2,1,0:T(8,128)(2,1)S(1)}, bf16[2,8,8,128]{3,2,1,0:T(8,128)(2,1)S(1)}, u32[]{:S(2)}, u32[]{:S(2)}) %collective-permute-start.3) | collective-permute-done | bytes 32800 | tf_op jit(solution)/shard_map/ppermute | solution.py:207
  22.3 0.4 %collective-permute-done.2 = bf16[2,8,8,128]{3,2,1,0:T(8,128)(2,1)S(1)} collective-permute-done((bf16[2,8,8,128]{3,2,1,0:T(8,128)(2,1)S(1)}, bf16[2,8,8,128]{3,2,1,0:T(8,128)(2,1)S(1)}, u32[]{:S(2)}, u32[]{:S(2)}) %collective-permute-start.2) | collective-permute-done | bytes 32800 | tf_op jit(solution)/shard_map/ppermute | solution.py:207
  22.8 2.7 %collective-permute-start.5 = (bf16[1,8,8,128]{3,2,1,0:T(8,128)(2,1)S(1)}, bf16[1,8,8,128]{3,2,1,0:T(8,128)(2,1)S(1)}, u32[]{:S(2)}, u32[]{:S(2)}) collective-permute-start(bf16[1,8,8,128]{3,2,1,0:T(8,128)(2,1)S(1)} %dynamic-slice_convert_fusion), channel_id=1, source_target_pairs={{0,8},{1,9},{2,10},{3,11},{4,12},{5,13},{6,14},{7,15},{8,0},{9,1},... | collective-permute-start | bytes 49160 | tf_op jit(solution)/shard_map/ppermute | solution.py:207
  25.4 2.0 %collective-permute-done.5 = bf16[1,8,8,128]{3,2,1,0:T(8,128)(2,1)S(1)} collective-permute-done((bf16[1,8,8,128]{3,2,1,0:T(8,128)(2,1)S(1)}, bf16[1,8,8,128]{3,2,1,0:T(8,128)(2,1)S(1)}, u32[]{:S(2)}, u32[]{:S(2)}) %collective-permute-start.5) | collective-permute-done | bytes 16416 | tf_op jit(solution)/shard_map/ppermute | solution.py:207
  27.5 0.6 %add_bitcast_fusion = f32[8,8,128]{2,1,0:T(8,128)} fusion(bf16[1,8,8,128]{3,2,1,0:T(8,128)(2,1)S(1)} %collective-permute-done.5, f32[2,8,8,128]{3,2,1,0:T(8,128)S(1)} %fusion.1, s32[]{:T(128)S(6)} %select_n.46), kind=kLoop, calls=%fused_computation.10 | loop fusion | flops 16384 | bytes 81924 | tf_op jit(solution)/shard_map/squeeze | solution.py:259
  (4 shorter events, 0.1 us)
Async XLA Ops:
  5.1 6.5 %collective-permute-start = (bf16[8,64,128]{2,1,0:T(8,128)(2,1)S(1)}, bf16[8,64,128]{2,1,0:T(8,128)(2,1)S(1)}, u32[]{:S(2)}, u32[]{:S(2)}) collective-permute-start(bf16[8,64,128]{2,1,0:T(8,128)(2,1)S(1)} %get-tuple-element.12), channel_id=1, source_target_pairs={{0,16},{16,0},{1,17},{17,1},{2,18},{18,2},{3,19},{19,3},{4,20},{20... | collective-permute-start | bytes 393224 | tf_op jit(solution)/shard_map/ppermute | solution.py:225
  8.2 3.5 %copy-start = (bf16[8,128,128]{2,1,0:T(8,128)(2,1)S(1)}, bf16[8,128,128]{2,1,0:T(8,128)(2,1)}, u32[]{:S(2)}) copy-start(bf16[8,128,128]{2,1,0:T(8,128)(2,1)} %refs_1_.3) | copy-start | bytes 786436
  8.2 3.5 %copy-start.1 = (bf16[8,64,128]{2,1,0:T(8,128)(2,1)S(1)}, bf16[8,64,128]{2,1,0:T(8,128)(2,1)}, u32[]{:S(2)}) copy-start(bf16[8,64,128]{2,1,0:T(8,128)(2,1)} %refs_2_.3) | copy-start | bytes 393220
  8.2 3.5 %copy-start.2 = (s32[16]{0:T(128)S(1)}, s32[16]{0:T(128)}, u32[]{:S(2)}) copy-start(s32[16]{0:T(128)} %vib.1) | copy-start | bytes 196
  8.2 3.5 %copy-start.3 = (s32[64]{0:T(128)S(1)}, s32[64]{0:T(128)}, u32[]{:S(2)}) copy-start(s32[64]{0:T(128)} %param.12) | copy-start | bytes 772
  8.2 3.5 %copy-start.4 = (s32[64]{0:T(128)S(1)}, s32[64]{0:T(128)}, u32[]{:S(2)}) copy-start(s32[64]{0:T(128)} %param.13) | copy-start | bytes 772
  14.1 1.3 %collective-permute-start.1 = (bf16[8,8,8,128]{3,2,1,0:T(8,128)(2,1)S(1)}, bf16[8,8,8,128]{3,2,1,0:T(8,128)(2,1)S(1)}, u32[]{:S(2)}, u32[]{:S(2)}) collective-permute-start(bf16[8,8,8,128]{3,2,1,0:T(8,128)(2,1)S(1)} %get-tuple-element.15), channel_id=1, source_target_pairs={{0,1},{1,0},{2,3},{3,2},{4,5},{5,4},{6,7},{7,6},{8,9},{9,8},{10,11... | collective-permute-start | bytes 393224 | tf_op jit(solution)/shard_map/ppermute | solution.py:207
  15.5 4.9 %collective-permute-start.4 = (bf16[2,8,8,128]{3,2,1,0:T(8,128)(2,1)S(1)}, bf16[2,8,8,128]{3,2,1,0:T(8,128)(2,1)S(1)}, u32[]{:S(2)}, u32[]{:S(2)}) collective-permute-start(bf16[2,8,8,128]{3,2,1,0:T(8,128)(2,1)S(1)} %get-tuple-element.18), channel_id=1, source_target_pairs={{0,6},{1,7},{2,4},{3,5},{4,2},{5,3},{6,0},{7,1},{8,14},{9,15},{10,... | collective-permute-start | bytes 98312 | tf_op jit(solution)/shard_map/ppermute | solution.py:207
  18.4 3.9 %collective-permute-start.3 = (bf16[2,8,8,128]{3,2,1,0:T(8,128)(2,1)S(1)}, bf16[2,8,8,128]{3,2,1,0:T(8,128)(2,1)S(1)}, u32[]{:S(2)}, u32[]{:S(2)}) collective-permute-start(bf16[2,8,8,128]{3,2,1,0:T(8,128)(2,1)S(1)} %get-tuple-element.17), channel_id=1, source_target_pairs={{0,4},{1,5},{2,6},{3,7},{4,0},{5,1},{6,2},{7,3},{8,12},{9,13},{10,... | collective-permute-start | bytes 98312 | tf_op jit(solution)/shard_map/ppermute | solution.py:207
  18.8 3.9 %collective-permute-start.2 = (bf16[2,8,8,128]{3,2,1,0:T(8,128)(2,1)S(1)}, bf16[2,8,8,128]{3,2,1,0:T(8,128)(2,1)S(1)}, u32[]{:S(2)}, u32[]{:S(2)}) collective-permute-start(bf16[2,8,8,128]{3,2,1,0:T(8,128)(2,1)S(1)} %get-tuple-element.16), channel_id=1, source_target_pairs={{0,2},{1,3},{2,0},{3,1},{4,6},{5,7},{6,4},{7,5},{8,10},{9,11},{10,... | collective-permute-start | bytes 98312 | tf_op jit(solution)/shard_map/ppermute | solution.py:207
  22.8 4.7 %collective-permute-start.5 = (bf16[1,8,8,128]{3,2,1,0:T(8,128)(2,1)S(1)}, bf16[1,8,8,128]{3,2,1,0:T(8,128)(2,1)S(1)}, u32[]{:S(2)}, u32[]{:S(2)}) collective-permute-start(bf16[1,8,8,128]{3,2,1,0:T(8,128)(2,1)S(1)} %dynamic-slice_convert_fusion), channel_id=1, source_target_pairs={{0,8},{1,9},{2,10},{3,11},{4,12},{5,13},{6,14},{7,15},{8,0},{9,1},... | collective-permute-start | bytes 49160 | tf_op jit(solution)/shard_map/ppermute | solution.py:207

commit v4 on v3

--- a/solution.py
+++ b/solution.py
@@ -22,9 +22,16 @@
     return lax.broadcasted_iota(jnp.int32, shape, axis)
 
 
+def column(row):
+    size = row.shape[1]
+    eye = iota((size, size), 0) == iota((size, size), 1)
+    return jnp.sum(jnp.where(eye, jnp.broadcast_to(row.astype(F32), (size, size)), 0.0), axis=1, keepdims=True)
+
+
 def decode_kernel(*refs, step, first):
     if first:
-        vib, hadamard, pilots, records, out, held, signs_v, ordered, mix, skewed, mixed, shifted, sems, vib_s, pilots_v, backward = refs
+        (vib, hadamard, pilots, owner, live, records), (out, held, signs_v, ordered, weight) = refs[:6], refs[6:11]
+        mix, skewed, mixed, shifted, sems, vib_s, pilots_v, owner_v, live_v, backward = refs[11:]
     else:
         held, signs_v, ordered, out, mix, skewed, mixed, shifted = refs
     sweeps, channels, samples = held.shape
@@ -43,7 +50,7 @@
         return pltpu.make_async_copy(records.at[:, :, cols], held.at[:, :, cols], sems.at[k])
 
     if first:
-        small = [(hadamard, signs_v), (pilots, pilots_v), (vib, vib_s)]
+        small = [(hadamard, signs_v), (pilots, pilots_v), (vib, vib_s), (owner, owner_v), (live, live_v)]
         small = [pltpu.make_async_copy(x, y, sems.at[CHUNKS + i]) for i, (x, y) in enumerate(small)]
         for copy in small:
             copy.start()
@@ -75,6 +82,12 @@
         small[2].wait()
         for c in range(codes):
             ordered[pl.ds(c, 1), :] = backward[pl.ds(vib_s[c], 1), :]
+        small[3].wait()
+        small[4].wait()
+        owner_c, live_c = column(owner_v[...]), column(live_v[...])
+        for c in range(owned):
+            match = (owner_c == vib_s[mine * owned + c].astype(F32)).astype(F32)
+            weight[c] = jnp.broadcast_to(live_c * (0.25 + match), weight.shape[1:])
     made = 0
 
     def skew(upto):
@@ -121,17 +134,20 @@
         pltpu.VMEM((early, samples, lags), BF16),
     ]
     if first:
-        vib, hadamard, pilots, _ = inputs
+        vib, hadamard, pilots, owner, live, _ = inputs
         inputs = [pltpu.with_memory_space_constraint(x, pltpu.HBM) for x in inputs]
         out_shape += [
             pltpu.VMEM(shape, BF16),
             pltpu.VMEM(hadamard.shape, jnp.int32),
             pltpu.VMEM((codes, samples + lags), F32),
+            pltpu.VMEM((owned, channels, lags), F32),
         ]
         scratch += [
-            pltpu.SemaphoreType.DMA((CHUNKS + 3,)),
+            pltpu.SemaphoreType.DMA((CHUNKS + 5,)),
             pltpu.SMEM(vib.shape, jnp.int32),
             pltpu.VMEM(pilots.shape, BF16),
+            pltpu.VMEM(owner.shape, jnp.int32),
+            pltpu.VMEM(live.shape, jnp.int32),
             pltpu.VMEM((pilots.shape[0], samples + lags), F32),
         ]
     return pl.pallas_call(
@@ -146,18 +162,17 @@
     )(*inputs)
 
 
-def tail_kernel(vib, owner, live, own, *refs, parts, radix, norm, factor):
-    others, (filters, targets, responses, keep), sends, terms = refs[:parts], refs[parts : parts + 4], refs[parts + 4 : -1], refs[-1]
+def orders(size):
+    bits = list(range(1, size.bit_length() - 1))
+    swapped = list(bits)
+    for i in range(0, len(bits) - 1, 2):
+        swapped[i], swapped[i + 1] = bits[i + 1], bits[i]
+    return [0] + bits, [0] + swapped
+
+
+def tail_kernel(weight, own, *refs, parts, norm, factor):
+    others, (filters, targets, responses, keep, send, terms) = refs[:parts], refs[parts:]
     owned, channels, lags = own.shape
-    first_code = lax.axis_index("sweep") * owned
-    digit = lax.rem(lax.axis_index("recv"), radix)
-    eye = iota((channels, channels), 0) == iota((channels, channels), 1)
-
-    def column(row):
-        return jnp.sum(jnp.where(eye, jnp.broadcast_to(row.astype(F32), (channels, channels)), 0.0), axis=1, keepdims=True)
-
-    owner_col = column(owner[...])
-    live_col = column(live[...])
     shares, _, share_rows, _ = terms.shape
     for c in range(owned):
         partial = own[c]
@@ -166,46 +181,19 @@
         decoded = (norm * partial).astype(BF16)
         response = jnp.dot(decoded, filters[c], preferred_element_type=F32)
         responses[c] = response
-        match = (owner_col == vib[first_code + c].astype(F32)).astype(F32)
-        weight = live_col * (0.25 + match)
-        residual = (weight * (response - targets[c].astype(F32))).astype(BF16)
+        residual = (weight[c] * (response - targets[c].astype(F32))).astype(BF16)
         grad = factor * lax.dot_general(decoded, residual, (((0,), (0,)), ((), ())), preferred_element_type=F32)
         for d in range(shares):
             terms[d, c] = grad[d * share_rows : (d + 1) * share_rows]
-    for hi in range(shares // radix):
-        keep[hi] = terms[hi * radix + digit]
-        for k, send in enumerate(sends):
-            send[hi] = terms[hi * radix + peer(digit, k + 1, radix)].astype(BF16)
-
-
-def peer(digit, k, radix):
-    if radix & (radix - 1) == 0:
-        return digit ^ k
-    return lax.rem(digit + k, radix) if not isinstance(digit, int) else (digit + k) % radix
-
-
-def radices(size):
-    parts = []
-    for want in (2, 4):
-        if size % want == 0 and size > 1:
-            parts.append(want)
-            size //= want
-    while size > 1:
-        f = next(q for q in (2, 3, 5, 7, size) if size % q == 0)
-        parts.append(f)
-        size //= f
-    return parts or [1]
-
-
-def exchange(values, stride, radix, size):
-    got = []
-    for k, value in enumerate(values):
-        pairs = []
-        for i in range(size):
-            d = i // stride % radix
-            pairs.append((i, i + (peer(d, k + 1, radix) - d) * stride))
-        got.append(lax.ppermute(value, "recv", pairs))
-    return got
+    parity = lax.rem(lax.axis_index("recv"), 2)
+    even, odd = orders(shares)
+    for i in range(shares // 2):
+        places = [
+            sum(1 << bit for j, bit in enumerate(reversed(order[1:])) if i >> j & 1) for order in (even, odd)
+        ]
+        mine, other = (places[0] + (places[1] - places[0]) * p for p in (parity, 1 - parity))
+        keep[i] = terms[mine + parity]
+        send[i] = terms[other + 1 - parity].astype(BF16)
 
 
 def local(records, pilots, hadamard, code_vibrator, owner_map, live_mask, filters, targets):
@@ -215,47 +203,39 @@
     owned, lags, _ = filters.shape
     channels = records.shape[1]
     received = []
-    inputs = (code_vibrator, hadamard, pilots, records)
+    inputs = (code_vibrator, hadamard, pilots, owner_map.reshape(1, channels), live_mask.reshape(1, channels), records)
+    first = True
     for step in list(range(1, groups)) + [0]:
         dtype = BF16 if step else F32
-        part, *extra = decode(inputs, records.shape, owned, codes, lags, step, dtype, len(inputs) == 4)
-        if extra:
-            inputs = tuple(extra)
+        part, *extra = decode(inputs, records.shape, owned, codes, lags, step, dtype, first)
+        if first:
+            *inputs, weight = extra
+            first = False
         if step:
             received.append(lax.ppermute(part, "sweep", [(i, (i + step) % groups) for i in range(groups)]))
-    own = part
-    steps = radices(size)
     share_rows = lags // size
-    piece = (size // steps[0], owned, share_rows, lags)
-    outs = pl.pallas_call(
+    piece = (size // 2, owned, share_rows, lags)
+    responses, held, sent = pl.pallas_call(
         functools.partial(
-            tail_kernel,
-            parts=len(received),
-            radix=steps[0],
-            norm=1.0 / math.sqrt(codes),
-            factor=1.0 / math.sqrt(channels * size),
+            tail_kernel, parts=len(received), norm=1.0 / math.sqrt(codes), factor=1.0 / math.sqrt(channels * size)
         ),
-        out_shape=[jax.ShapeDtypeStruct((owned, channels, lags), F32), jax.ShapeDtypeStruct(piece, F32)]
-        + [jax.ShapeDtypeStruct(piece, BF16)] * (steps[0] - 1),
-        in_specs=[SMEM] + [VMEM] * (5 + len(received)),
-        out_specs=[VMEM] * (1 + steps[0]),
+        out_shape=[pltpu.VMEM((owned, channels, lags), F32), pltpu.VMEM(piece, F32), pltpu.VMEM(piece, BF16)],
+        in_specs=[VMEM] * (4 + len(received)),
+        out_specs=[VMEM] * 3,
         scratch_shapes=[pltpu.VMEM((size, owned, share_rows, lags), F32)],
-        compiler_params=pltpu.CompilerParams(vmem_limit_bytes=4 * 2**20),
+        compiler_params=pltpu.CompilerParams(vmem_limit_bytes=8 * 2**20),
         name="tail",
-    )(code_vibrator, owner_map.reshape(1, channels), live_mask.reshape(1, channels), own, *received, filters, targets)
-    responses, held, sends = outs[0], outs[1], outs[2:]
+    )(weight, part, *received, filters, targets)
     me = lax.axis_index("recv")
-    stride = 1
-    for radix, after in zip(steps, steps[1:] + [None]):
-        for got in exchange(sends, stride, radix, size):
-            held = held + got.astype(F32)
-        stride *= radix
-        if after is None:
-            break
-        digit = me // stride % after
-        grid = held.reshape((held.shape[0] // after, after) + held.shape[1:])
-        sends = [lax.dynamic_index_in_dim(grid, peer(digit, k, after), 1, keepdims=False).astype(BF16) for k in range(1, after)]
-        held = lax.dynamic_index_in_dim(grid, digit, 1, keepdims=False)
+    even, odd = orders(size)
+    for j in range(len(even)):
+        pairs = [(i, i ^ (1 << (odd if i & 1 else even)[j])) for i in range(size)]
+        held = held + lax.ppermute(sent, "recv", pairs).astype(F32)
+        if j + 1 < len(even):
+            bit = jnp.where(me & 1 == 1, me >> odd[j + 1], me >> even[j + 1]) & 1
+            half = held.shape[0] // 2
+            sent = lax.dynamic_slice_in_dim(held, (1 - bit) * half, half, 0).astype(BF16)
+            held = lax.dynamic_slice_in_dim(held, bit * half, half, 0)
     return (responses, held[0])
 
 

time: 28.3 us -> 28.5 us (level)
  Pallas kernels: 9.76 us -> 8.74 us
  local copies, waits for them, and re-layouts: 0.06 us -> 0.76 us
  starting transfers between devices: 9.23 us -> 9.74 us
    pallas_call x1, Pallas kernels: 2.41 us -> 1.34 us  [local(): pl.pallas_call(functools.partial(tail_kernel, parts=len(received), norm=1...]
    unnamed x10 -> x5, local copies, waits for them, and re-layouts: 0.02 us -> 0.71 us
    ppermute x5 -> x4, starting transfers between devices: 6.21 us -> 6.7 us  [local(): held = held + lax.ppermute(sent, 'recv', pairs).astype(F32)]
    ppermute x5 -> x4, waiting for transfers between devices: 7.05 us -> 7.01 us  [local(): held = held + lax.ppermute(sent, 'recv', pairs).astype(F32)]
  transfers between devices with their start and end apart: 6 -> 5, of which waited for: 6 -> 5; matrix products, arithmetic and copies ran while one was open for 0% -> 2% of each run, Pallas kernels for 10% -> 10%
where the time goes in v4:
time: 28.5 us; the launch traced here: 28.3 us
  starting transfers between devices  9.74 us (34%)
  Pallas kernels  8.74 us (31%)
  waiting for transfers between devices  7.65 us (27%)
  local copies, waits for them, and re-layouts  0.76 us (3%)
  between operations  0.71 us (2%)
  other arithmetic  0.67 us (2%)
    pallas_call x2, Pallas kernels, decode(): pl.pallas_call(functools.partial(decode_kernel, step=step, first=first),...  7.4 us
    ppermute x4, waiting for transfers between devices, local(): held = held + lax.ppermute(sent, 'recv', pairs).astype(F32)  7.01 us
    ppermute x4, starting transfers between devices, local(): held = held + lax.ppermute(sent, 'recv', pairs).astype(F32)  6.7 us
    ppermute x1, starting transfers between devices, local(): lax.ppermute(part, 'sweep', [(i, (i + step) % groups) for i in range(grou...  3.04 us
    pallas_call x1, Pallas kernels, local(): pl.pallas_call(functools.partial(tail_kernel, parts=len(received), norm=1...  1.34 us
    unnamed x5, local copies, waits for them, and re-layouts  0.71 us
    ppermute x1, waiting for transfers between devices, local(): lax.ppermute(part, 'sweep', [(i, (i + step) % groups) for i in range(grou...  0.64 us
    squeeze x1, other arithmetic, local(): return (responses, held[0])  0.62 us
  transfers between devices with their start and end apart: 5, of which 5 were waited for; matrix products, arithmetic and copies ran while one was open for 2% of the time, Pallas kernels for 10%

profile of v4, /device:TPU:0, one launch (start us, length us, event | category | flops | bytes accessed | tf_op | source)
XLA Modules:
  0.0 28.3 jit_solution(710966304150494309)
XLA Ops:
  0.6 4.6 %decode_1.1 = (bf16[8,64,128]{2,1,0:T(8,128)(2,1)S(1)}, bf16[8,64,4096]{2,1,0:T(8,128)(2,1)S(1)}, s32[16,16]{1,0:T(8,128)S(1)}, f32[16,4224]{1,0:T(8,128)S(1)}, f32[8,64,128]{2,1,0:T(8,128)S(1)}) custom-call(s32[16]{0:T(128)} %refs_0_.1, s32[16,16]{1,0:T(8,128)} %refs_1_.2, bf16[16,3968]{1,0:T(8,128)(2,1)} %refs_2_.2, s32[1,64]{1,0:T(1,128)} %bitcast.4, ...), custom_call_target="tpu_custom_call" | custom-call | flops 8000000000 | bytes 4194304 | tf_op jit(solution)/shard_map/decode_1/pallas_call | solution.py:153
  5.2 3.0 %collective-permute-start = (bf16[8,64,128]{2,1,0:T(8,128)(2,1)S(1)}, bf16[8,64,128]{2,1,0:T(8,128)(2,1)S(1)}, u32[]{:S(2)}, u32[]{:S(2)}) collective-permute-start(bf16[8,64,128]{2,1,0:T(8,128)(2,1)S(1)} %get-tuple-element.14), channel_id=1, source_target_pairs={{0,16},{16,0},{1,17},{17,1},{2,18},{18,2},{3,19},{19,3},{4,20},{20... | collective-permute-start | bytes 393224 | tf_op jit(solution)/shard_map/ppermute | solution.py:215
  8.2 0.0 copy-start
  8.2 0.0 copy-start.1
  8.2 2.8 %decode_0.1.own = f32[8,64,128]{2,1,0:T(8,128)S(1)} custom-call(bf16[8,64,4096]{2,1,0:T(8,128)(2,1)S(1)} %get-tuple-element.11.refs_0_, s32[16,16]{1,0:T(8,128)S(1)} %get-tuple-element.12.refs_1_, f32[16,4224]{1,0:T(8,128)S(1)} %get-tuple-element.13.refs_2_), custom_call_target="tpu_custom_call" | custom-call | flops 8000000000 | bytes 4194304 | tf_op jit(solution)/shard_map/decode_0/pallas_call | solution.py:153
  11.1 0.6 %collective-permute-done.refs_0_ = bf16[8,64,128]{2,1,0:T(8,128)(2,1)S(1)} collective-permute-done((bf16[8,64,128]{2,1,0:T(8,128)(2,1)S(1)}, bf16[8,64,128]{2,1,0:T(8,128)(2,1)S(1)}, u32[]{:S(2)}, u32[]{:S(2)}) %collective-permute-start) | collective-permute-done | bytes 131104 | tf_op jit(solution)/shard_map/ppermute | solution.py:215
  11.7 0.0 copy-done
  11.7 0.0 copy-done.1
  11.7 1.3 %tail.1 = (f32[8,64,128]{2,1,0:T(8,128)S(1)}, f32[8,8,8,128]{3,2,1,0:T(8,128)S(1)}, bf16[8,8,8,128]{3,2,1,0:T(8,128)(2,1)S(1)}) custom-call(f32[8,64,128]{2,1,0:T(8,128)S(1)} %get-tuple-element.10.weight, f32[8,64,128]{2,1,0:T(8,128)S(1)} %decode_0.1.own, bf16[8,64,128]{2,1,0:T(8,128)(2,1)S(1)} %collective-permute-done.refs_0_, ...), custom_call_target="tpu_custom_call" | custom-call | tf_op jit(solution)/shard_map/tail/pallas_call | solution.py:218
  13.1 0.1 collective-permute-start.1
  13.2 1.3 %collective-permute-done.1 = bf16[8,8,8,128]{3,2,1,0:T(8,128)(2,1)S(1)} collective-permute-done((bf16[8,8,8,128]{3,2,1,0:T(8,128)(2,1)S(1)}, bf16[8,8,8,128]{3,2,1,0:T(8,128)(2,1)S(1)}, u32[]{:S(2)}, u32[]{:S(2)}) %collective-permute-start.1) | collective-permute-done | bytes 131104 | tf_op jit(solution)/shard_map/ppermute | solution.py:233
  14.6 1.8 %collective-permute-start.2 = (bf16[4,8,8,128]{3,2,1,0:T(8,128)(2,1)S(1)}, bf16[4,8,8,128]{3,2,1,0:T(8,128)(2,1)S(1)}, u32[]{:S(2)}, u32[]{:S(2)}) collective-permute-start(bf16[4,8,8,128]{3,2,1,0:T(8,128)(2,1)S(1)} %dynamic-slice_convert_fusion), channel_id=1, source_target_pairs={{0,2},{1,5},{2,0},{3,7},{4,6},{5,1},{6,4},{7,3},{8,10},{9,13},{10,... | collective-permute-start | bytes 196616 | tf_op jit(solution)/shard_map/ppermute | solution.py:233
  16.4 2.5 %collective-permute-done.2 = bf16[4,8,8,128]{3,2,1,0:T(8,128)(2,1)S(1)} collective-permute-done((bf16[4,8,8,128]{3,2,1,0:T(8,128)(2,1)S(1)}, bf16[4,8,8,128]{3,2,1,0:T(8,128)(2,1)S(1)}, u32[]{:S(2)}, u32[]{:S(2)}) %collective-permute-start.2) | collective-permute-done | bytes 65568 | tf_op jit(solution)/shard_map/ppermute | solution.py:233
  18.9 1.9 %collective-permute-start.3 = (bf16[2,8,8,128]{3,2,1,0:T(8,128)(2,1)S(1)}, bf16[2,8,8,128]{3,2,1,0:T(8,128)(2,1)S(1)}, u32[]{:S(2)}, u32[]{:S(2)}) collective-permute-start(bf16[2,8,8,128]{3,2,1,0:T(8,128)(2,1)S(1)} %dynamic-slice_convert_fusion.1), channel_id=1, source_target_pairs={{0,4},{1,3},{2,6},{3,1},{4,0},{5,7},{6,2},{7,5},{8,12},{9,11},{10,... | collective-permute-start | bytes 98312 | tf_op jit(solution)/shard_map/ppermute | solution.py:233
  20.8 2.1 %collective-permute-done.3 = bf16[2,8,8,128]{3,2,1,0:T(8,128)(2,1)S(1)} collective-permute-done((bf16[2,8,8,128]{3,2,1,0:T(8,128)(2,1)S(1)}, bf16[2,8,8,128]{3,2,1,0:T(8,128)(2,1)S(1)}, u32[]{:S(2)}, u32[]{:S(2)}) %collective-permute-start.3) | collective-permute-done | bytes 32800 | tf_op jit(solution)/shard_map/ppermute | solution.py:233
  22.9 2.9 %collective-permute-start.4 = (bf16[1,8,8,128]{3,2,1,0:T(8,128)(2,1)S(1)}, bf16[1,8,8,128]{3,2,1,0:T(8,128)(2,1)S(1)}, u32[]{:S(2)}, u32[]{:S(2)}) collective-permute-start(bf16[1,8,8,128]{3,2,1,0:T(8,128)(2,1)S(1)} %dynamic-slice_convert_fusion.2), channel_id=1, source_target_pairs={{0,8},{1,9},{2,10},{3,11},{4,12},{5,13},{6,14},{7,15},{8,0},{9,1},... | collective-permute-start | bytes 49160 | tf_op jit(solution)/shard_map/ppermute | solution.py:233
  25.8 0.7 %copy.10 = f32[8,64,128]{2,1,0:T(8,128)} copy(f32[8,64,128]{2,1,0:T(8,128)S(1)} %get-tuple-element.18) | data formatting | bytes 524288
  26.5 1.1 %collective-permute-done.4 = bf16[1,8,8,128]{3,2,1,0:T(8,128)(2,1)S(1)} collective-permute-done((bf16[1,8,8,128]{3,2,1,0:T(8,128)(2,1)S(1)}, bf16[1,8,8,128]{3,2,1,0:T(8,128)(2,1)S(1)}, u32[]{:S(2)}, u32[]{:S(2)}) %collective-permute-start.4) | collective-permute-done | bytes 16416 | tf_op jit(solution)/shard_map/ppermute | solution.py:233
  27.6 0.6 %add_bitcast_fusion = f32[8,8,128]{2,1,0:T(8,128)} fusion(bf16[1,8,8,128]{3,2,1,0:T(8,128)(2,1)S(1)} %collective-permute-done.4, f32[2,8,8,128]{3,2,1,0:T(8,128)S(1)} %convert_add_fusion.2, s32[]{:T(128)S(6)} %select_n.32), kind=kLoop, calls=%fused_computation.5 | loop fusion | flops 16384 | bytes 81924 | tf_op jit(solution)/shard_map/squeeze | solution.py:239
  (6 shorter events, 0.1 us)
Async XLA Ops:
  5.2 6.5 %collective-permute-start = (bf16[8,64,128]{2,1,0:T(8,128)(2,1)S(1)}, bf16[8,64,128]{2,1,0:T(8,128)(2,1)S(1)}, u32[]{:S(2)}, u32[]{:S(2)}) collective-permute-start(bf16[8,64,128]{2,1,0:T(8,128)(2,1)S(1)} %get-tuple-element.14), channel_id=1, source_target_pairs={{0,16},{16,0},{1,17},{17,1},{2,18},{18,2},{3,19},{19,3},{4,20},{20... | collective-permute-start | bytes 393224 | tf_op jit(solution)/shard_map/ppermute | solution.py:215
  8.2 3.5 %copy-start = (bf16[8,128,128]{2,1,0:T(8,128)(2,1)S(1)}, bf16[8,128,128]{2,1,0:T(8,128)(2,1)}, u32[]{:S(2)}) copy-start(bf16[8,128,128]{2,1,0:T(8,128)(2,1)} %refs_1_.3) | copy-start | bytes 786436
  8.2 3.5 %copy-start.1 = (bf16[8,64,128]{2,1,0:T(8,128)(2,1)S(1)}, bf16[8,64,128]{2,1,0:T(8,128)(2,1)}, u32[]{:S(2)}) copy-start(bf16[8,64,128]{2,1,0:T(8,128)(2,1)} %refs_2_.3) | copy-start | bytes 393220
  13.1 1.4 %collective-permute-start.1 = (bf16[8,8,8,128]{3,2,1,0:T(8,128)(2,1)S(1)}, bf16[8,8,8,128]{3,2,1,0:T(8,128)(2,1)S(1)}, u32[]{:S(2)}, u32[]{:S(2)}) collective-permute-start(bf16[8,8,8,128]{3,2,1,0:T(8,128)(2,1)S(1)} %get-tuple-element.17), channel_id=1, source_target_pairs={{0,1},{1,0},{2,3},{3,2},{4,5},{5,4},{6,7},{7,6},{8,9},{9,8},{10,11... | collective-permute-start | bytes 393224 | tf_op jit(solution)/shard_map/ppermute | solution.py:233
  14.6 4.3 %collective-permute-start.2 = (bf16[4,8,8,128]{3,2,1,0:T(8,128)(2,1)S(1)}, bf16[4,8,8,128]{3,2,1,0:T(8,128)(2,1)S(1)}, u32[]{:S(2)}, u32[]{:S(2)}) collective-permute-start(bf16[4,8,8,128]{3,2,1,0:T(8,128)(2,1)S(1)} %dynamic-slice_convert_fusion), channel_id=1, source_target_pairs={{0,2},{1,5},{2,0},{3,7},{4,6},{5,1},{6,4},{7,3},{8,10},{9,13},{10,... | collective-permute-start | bytes 196616 | tf_op jit(solution)/shard_map/ppermute | solution.py:233
  18.9 4.0 %collective-permute-start.3 = (bf16[2,8,8,128]{3,2,1,0:T(8,128)(2,1)S(1)}, bf16[2,8,8,128]{3,2,1,0:T(8,128)(2,1)S(1)}, u32[]{:S(2)}, u32[]{:S(2)}) collective-permute-start(bf16[2,8,8,128]{3,2,1,0:T(8,128)(2,1)S(1)} %dynamic-slice_convert_fusion.1), channel_id=1, source_target_pairs={{0,4},{1,3},{2,6},{3,1},{4,0},{5,7},{6,2},{7,5},{8,12},{9,11},{10,... | collective-permute-start | bytes 98312 | tf_op jit(solution)/shard_map/ppermute | solution.py:233
  22.9 4.7 %collective-permute-start.4 = (bf16[1,8,8,128]{3,2,1,0:T(8,128)(2,1)S(1)}, bf16[1,8,8,128]{3,2,1,0:T(8,128)(2,1)S(1)}, u32[]{:S(2)}, u32[]{:S(2)}) collective-permute-start(bf16[1,8,8,128]{3,2,1,0:T(8,128)(2,1)S(1)} %dynamic-slice_convert_fusion.2), channel_id=1, source_target_pairs={{0,8},{1,9},{2,10},{3,11},{4,12},{5,13},{6,14},{7,15},{8,0},{9,1},... | collective-permute-start | bytes 49160 | tf_op jit(solution)/shard_map/ppermute | solution.py:233

commit v5 on v4

--- a/solution.py
+++ b/solution.py
@@ -162,38 +162,38 @@
     )(*inputs)
 
 
-def orders(size):
-    bits = list(range(1, size.bit_length() - 1))
-    swapped = list(bits)
-    for i in range(0, len(bits) - 1, 2):
-        swapped[i], swapped[i + 1] = bits[i + 1], bits[i]
-    return [0] + bits, [0] + swapped
-
-
-def tail_kernel(weight, own, *refs, parts, norm, factor):
-    others, (filters, targets, responses, keep, send, terms) = refs[:parts], refs[parts:]
-    owned, channels, lags = own.shape
+def tail_kernel(weight, own, *refs, parts, norm, factor, radix):
+    others, (filters, targets, responses, keep, *sends, terms) = refs[:parts], refs[parts:]
+    owned = own.shape[0]
     shares, _, share_rows, _ = terms.shape
-    for c in range(owned):
-        partial = own[c]
-        for other in others:
-            partial = partial + other[c].astype(F32)
-        decoded = (norm * partial).astype(BF16)
-        response = jnp.dot(decoded, filters[c], preferred_element_type=F32)
-        responses[c] = response
-        residual = (weight[c] * (response - targets[c].astype(F32))).astype(BF16)
-        grad = factor * lax.dot_general(decoded, residual, (((0,), (0,)), ((), ())), preferred_element_type=F32)
+    every = range(owned)
+    partial = [own[c] for c in every]
+    for other in others:
+        partial = [partial[c] + other[c].astype(F32) for c in every]
+    decoded = [(norm * p).astype(BF16) for p in partial]
+    response = [jnp.dot(decoded[c], filters[c], preferred_element_type=F32) for c in every]
+    for c in every:
+        responses[c] = response[c]
+    residual = [(weight[c] * (response[c] - targets[c].astype(F32))).astype(BF16) for c in every]
+    grad = [
+        factor * lax.dot_general(decoded[c], residual[c], (((0,), (0,)), ((), ())), preferred_element_type=F32)
+        for c in every
+    ]
+    for c in every:
         for d in range(shares):
-            terms[d, c] = grad[d * share_rows : (d + 1) * share_rows]
-    parity = lax.rem(lax.axis_index("recv"), 2)
-    even, odd = orders(shares)
-    for i in range(shares // 2):
-        places = [
-            sum(1 << bit for j, bit in enumerate(reversed(order[1:])) if i >> j & 1) for order in (even, odd)
-        ]
-        mine, other = (places[0] + (places[1] - places[0]) * p for p in (parity, 1 - parity))
-        keep[i] = terms[mine + parity]
-        send[i] = terms[other + 1 - parity].astype(BF16)
+            terms[d, c] = grad[c][d * share_rows : (d + 1) * share_rows]
+    digit = lax.rem(lax.axis_index("recv"), radix)
+    for i in range(shares // radix):
+        keep[i] = terms[i * radix + digit]
+        for k, send in enumerate(sends):
+            send[i] = terms[i * radix + (digit ^ (k + 1))].astype(BF16)
+
+
+def rounds(size):
+    parts = [2]
+    while math.prod(parts) < size:
+        parts.append(4 if size // math.prod(parts) % 4 == 0 else 2)
+    return parts
 
 
 def local(records, pilots, hadamard, code_vibrator, owner_map, live_mask, filters, targets):
@@ -214,28 +214,39 @@
         if step:
             received.append(lax.ppermute(part, "sweep", [(i, (i + step) % groups) for i in range(groups)]))
     share_rows = lags // size
-    piece = (size // 2, owned, share_rows, lags)
-    responses, held, sent = pl.pallas_call(
+    radices = rounds(size)
+    piece = (size // radices[0], owned, share_rows, lags)
+    responses, held, *sent = pl.pallas_call(
         functools.partial(
-            tail_kernel, parts=len(received), norm=1.0 / math.sqrt(codes), factor=1.0 / math.sqrt(channels * size)
+            tail_kernel,
+            parts=len(received),
+            norm=1.0 / math.sqrt(codes),
+            factor=1.0 / math.sqrt(channels * size),
+            radix=radices[0],
         ),
-        out_shape=[pltpu.VMEM((owned, channels, lags), F32), pltpu.VMEM(piece, F32), pltpu.VMEM(piece, BF16)],
+        out_shape=[pltpu.VMEM((owned, channels, lags), F32), pltpu.VMEM(piece, F32)]
+        + [pltpu.VMEM(piece, BF16)] * (radices[0] - 1),
         in_specs=[VMEM] * (4 + len(received)),
-        out_specs=[VMEM] * 3,
+        out_specs=[VMEM] * (1 + radices[0]),
         scratch_shapes=[pltpu.VMEM((size, owned, share_rows, lags), F32)],
         compiler_params=pltpu.CompilerParams(vmem_limit_bytes=8 * 2**20),
         name="tail",
     )(weight, part, *received, filters, targets)
     me = lax.axis_index("recv")
-    even, odd = orders(size)
-    for j in range(len(even)):
-        pairs = [(i, i ^ (1 << (odd if i & 1 else even)[j])) for i in range(size)]
-        held = held + lax.ppermute(sent, "recv", pairs).astype(F32)
-        if j + 1 < len(even):
-            bit = jnp.where(me & 1 == 1, me >> odd[j + 1], me >> even[j + 1]) & 1
-            half = held.shape[0] // 2
-            sent = lax.dynamic_slice_in_dim(held, (1 - bit) * half, half, 0).astype(BF16)
-            held = lax.dynamic_slice_in_dim(held, bit * half, half, 0)
+    stride = 1
+    for j, radix in enumerate(radices):
+        for k, value in enumerate(sent):
+            pairs = [(i, i ^ (k + 1) * stride) for i in range(size)]
+            held = held + lax.ppermute(value, "recv", pairs).astype(F32)
+        stride *= radix
+        if j + 1 < len(radices):
+            digit = (me // stride) & (radices[j + 1] - 1)
+            grid = held.reshape((-1, radices[j + 1]) + held.shape[1:])
+            sent = [
+                lax.dynamic_index_in_dim(grid, digit ^ k, 1, keepdims=False).astype(BF16)
+                for k in range(1, radices[j + 1])
+            ]
+            held = lax.dynamic_index_in_dim(grid, digit, 1, keepdims=False)
     return (responses, held[0])
 
 

time: 28.5 us -> 26.4 us (0.926)
  Pallas kernels: 8.74 us -> 7.8 us
  waiting for transfers between devices: 7.65 us -> 6.95 us
  starting transfers between devices: 9.74 us -> 9.31 us
    pallas_call x1, Pallas kernels: 1.34 us -> 0.4 us  [local(): pl.pallas_call(functools.partial(tail_kernel, parts=len(received), norm=1...]
    ppermute x4 -> x5, waiting for transfers between devices: 7.01 us -> 6.31 us  [local(): held = held + lax.ppermute(value, 'recv', pairs).astype(F32)]
    ppermute x4 -> x5, starting transfers between devices: 6.7 us -> 6.27 us  [local(): held = held + lax.ppermute(value, 'recv', pairs).astype(F32)]
  transfers between devices with their start and end apart: 5 -> 6, of which waited for: 5 -> 6; matrix products, arithmetic and copies ran while one was open for 2% -> 3% of each run, Pallas kernels for 10% -> 11%
where the time goes in v5:
time: 26.4 us; the launch traced here: 26.2 us
  starting transfers between devices  9.31 us (35%)
  Pallas kernels  7.8 us (30%)
  waiting for transfers between devices  6.95 us (26%)
  local copies, waits for them, and re-layouts  0.75 us (3%)
  between operations  0.72 us (3%)
  other arithmetic  0.66 us (2%)
    pallas_call x2, Pallas kernels, decode(): pl.pallas_call(functools.partial(decode_kernel, step=step, first=first),...  7.4 us
    ppermute x5, waiting for transfers between devices, local(): held = held + lax.ppermute(value, 'recv', pairs).astype(F32)  6.31 us
    ppermute x5, starting transfers between devices, local(): held = held + lax.ppermute(value, 'recv', pairs).astype(F32)  6.27 us
    ppermute x1, starting transfers between devices, local(): lax.ppermute(part, 'sweep', [(i, (i + step) % groups) for i in range(grou...  3.04 us
    unnamed x5, local copies, waits for them, and re-layouts  0.71 us
    ppermute x1, waiting for transfers between devices, local(): lax.ppermute(part, 'sweep', [(i, (i + step) % groups) for i in range(grou...  0.64 us
    squeeze x1, other arithmetic, local(): return (responses, held[0])  0.62 us
  transfers between devices with their start and end apart: 6, of which 6 were waited for; matrix products, arithmetic and copies ran while one was open for 3% of the time, Pallas kernels for 11%

profile of v5, /device:TPU:0, one launch (start us, length us, event | category | flops | bytes accessed | tf_op | source)
XLA Modules:
  0.0 26.2 jit_solution(10728483042770110929)
XLA Ops:
  0.6 4.6 %decode_1.1 = (bf16[8,64,128]{2,1,0:T(8,128)(2,1)S(1)}, bf16[8,64,4096]{2,1,0:T(8,128)(2,1)S(1)}, s32[16,16]{1,0:T(8,128)S(1)}, f32[16,4224]{1,0:T(8,128)S(1)}, f32[8,64,128]{2,1,0:T(8,128)S(1)}) custom-call(s32[16]{0:T(128)} %refs_0_.1, s32[16,16]{1,0:T(8,128)} %refs_1_.2, bf16[16,3968]{1,0:T(8,128)(2,1)} %refs_2_.2, s32[1,64]{1,0:T(1,128)} %bitcast.31, ...), custom_call_target="tpu_custom_call" | custom-call | flops 8000000000 | bytes 4194304 | tf_op jit(solution)/shard_map/decode_1/pallas_call | solution.py:153
  5.2 3.0 %collective-permute-start = (bf16[8,64,128]{2,1,0:T(8,128)(2,1)S(1)}, bf16[8,64,128]{2,1,0:T(8,128)(2,1)S(1)}, u32[]{:S(2)}, u32[]{:S(2)}) collective-permute-start(bf16[8,64,128]{2,1,0:T(8,128)(2,1)S(1)} %get-tuple-element.14), channel_id=1, source_target_pairs={{0,16},{16,0},{1,17},{17,1},{2,18},{18,2},{3,19},{19,3},{4,20},{20... | collective-permute-start | bytes 393224 | tf_op jit(solution)/shard_map/ppermute | solution.py:215
  8.2 0.0 copy-start
  8.2 0.0 copy-start.1
  8.2 2.8 %decode_0.1.own = f32[8,64,128]{2,1,0:T(8,128)S(1)} custom-call(bf16[8,64,4096]{2,1,0:T(8,128)(2,1)S(1)} %get-tuple-element.11.refs_0_, s32[16,16]{1,0:T(8,128)S(1)} %get-tuple-element.12.refs_1_, f32[16,4224]{1,0:T(8,128)S(1)} %get-tuple-element.13.refs_2_), custom_call_target="tpu_custom_call" | custom-call | flops 8000000000 | bytes 4194304 | tf_op jit(solution)/shard_map/decode_0/pallas_call | solution.py:153
  11.1 0.6 %collective-permute-done.refs_0_ = bf16[8,64,128]{2,1,0:T(8,128)(2,1)S(1)} collective-permute-done((bf16[8,64,128]{2,1,0:T(8,128)(2,1)S(1)}, bf16[8,64,128]{2,1,0:T(8,128)(2,1)S(1)}, u32[]{:S(2)}, u32[]{:S(2)}) %collective-permute-start) | collective-permute-done | bytes 131104 | tf_op jit(solution)/shard_map/ppermute | solution.py:215
  11.7 0.0 copy-done
  11.7 0.0 copy-done.1
  11.7 0.4 %tail.1 = (f32[8,64,128]{2,1,0:T(8,128)S(1)}, f32[8,8,8,128]{3,2,1,0:T(8,128)S(1)}, bf16[8,8,8,128]{3,2,1,0:T(8,128)(2,1)S(1)}) custom-call(f32[8,64,128]{2,1,0:T(8,128)S(1)} %get-tuple-element.10.weight, f32[8,64,128]{2,1,0:T(8,128)S(1)} %decode_0.1.own, bf16[8,64,128]{2,1,0:T(8,128)(2,1)S(1)} %collective-permute-done.refs_0_, ...), custom_call_target="tpu_custom_call" | custom-call | tf_op jit(solution)/shard_map/tail/pallas_call | solution.py:219
  12.1 0.1 collective-permute-start.1
  12.3 1.3 %collective-permute-done.1 = bf16[8,8,8,128]{3,2,1,0:T(8,128)(2,1)S(1)} collective-permute-done((bf16[8,8,8,128]{3,2,1,0:T(8,128)(2,1)S(1)}, bf16[8,8,8,128]{3,2,1,0:T(8,128)(2,1)S(1)}, u32[]{:S(2)}, u32[]{:S(2)}) %collective-permute-start.1) | collective-permute-done | bytes 131104 | tf_op jit(solution)/shard_map/ppermute | solution.py:240
  13.6 2.8 %collective-permute-start.4 = (bf16[2,8,8,128]{3,2,1,0:T(8,128)(2,1)S(1)}, bf16[2,8,8,128]{3,2,1,0:T(8,128)(2,1)S(1)}, u32[]{:S(2)}, u32[]{:S(2)}) collective-permute-start(bf16[2,8,8,128]{3,2,1,0:T(8,128)(2,1)S(1)} %get-tuple-element.20), channel_id=1, source_target_pairs={{0,6},{1,7},{2,4},{3,5},{4,2},{5,3},{6,0},{7,1},{8,14},{9,15},{10,... | collective-permute-start | bytes 98312 | tf_op jit(solution)/shard_map/ppermute | solution.py:240
  16.5 0.5 %collective-permute-start.3 = (bf16[2,8,8,128]{3,2,1,0:T(8,128)(2,1)S(1)}, bf16[2,8,8,128]{3,2,1,0:T(8,128)(2,1)S(1)}, u32[]{:S(2)}, u32[]{:S(2)}) collective-permute-start(bf16[2,8,8,128]{3,2,1,0:T(8,128)(2,1)S(1)} %get-tuple-element.19), channel_id=1, source_target_pairs={{0,4},{1,5},{2,6},{3,7},{4,0},{5,1},{6,2},{7,3},{8,12},{9,13},{10,... | collective-permute-start | bytes 98312 | tf_op jit(solution)/shard_map/ppermute | solution.py:240
  16.9 0.3 collective-permute-start.2
  17.2 1.3 %collective-permute-done.4 = bf16[2,8,8,128]{3,2,1,0:T(8,128)(2,1)S(1)} collective-permute-done((bf16[2,8,8,128]{3,2,1,0:T(8,128)(2,1)S(1)}, bf16[2,8,8,128]{3,2,1,0:T(8,128)(2,1)S(1)}, u32[]{:S(2)}, u32[]{:S(2)}) %collective-permute-start.4) | collective-permute-done | bytes 32800 | tf_op jit(solution)/shard_map/ppermute | solution.py:240
  18.5 1.9 %collective-permute-done.3 = bf16[2,8,8,128]{3,2,1,0:T(8,128)(2,1)S(1)} collective-permute-done((bf16[2,8,8,128]{3,2,1,0:T(8,128)(2,1)S(1)}, bf16[2,8,8,128]{3,2,1,0:T(8,128)(2,1)S(1)}, u32[]{:S(2)}, u32[]{:S(2)}) %collective-permute-start.3) | collective-permute-done | bytes 32800 | tf_op jit(solution)/shard_map/ppermute | solution.py:240
  20.4 0.5 %collective-permute-done.2 = bf16[2,8,8,128]{3,2,1,0:T(8,128)(2,1)S(1)} collective-permute-done((bf16[2,8,8,128]{3,2,1,0:T(8,128)(2,1)S(1)}, bf16[2,8,8,128]{3,2,1,0:T(8,128)(2,1)S(1)}, u32[]{:S(2)}, u32[]{:S(2)}) %collective-permute-start.2) | collective-permute-done | bytes 32800 | tf_op jit(solution)/shard_map/ppermute | solution.py:240
  20.9 2.6 %collective-permute-start.5 = (bf16[1,8,8,128]{3,2,1,0:T(8,128)(2,1)S(1)}, bf16[1,8,8,128]{3,2,1,0:T(8,128)(2,1)S(1)}, u32[]{:S(2)}, u32[]{:S(2)}) collective-permute-start(bf16[1,8,8,128]{3,2,1,0:T(8,128)(2,1)S(1)} %dynamic-slice_convert_fusion), channel_id=1, source_target_pairs={{0,8},{1,9},{2,10},{3,11},{4,12},{5,13},{6,14},{7,15},{8,0},{9,1},... | collective-permute-start | bytes 49160 | tf_op jit(solution)/shard_map/ppermute | solution.py:240
  23.5 0.7 %copy.16 = f32[8,64,128]{2,1,0:T(8,128)} copy(f32[8,64,128]{2,1,0:T(8,128)S(1)} %get-tuple-element.21) | data formatting | bytes 524288
  24.2 1.4 %collective-permute-done.5 = bf16[1,8,8,128]{3,2,1,0:T(8,128)(2,1)S(1)} collective-permute-done((bf16[1,8,8,128]{3,2,1,0:T(8,128)(2,1)S(1)}, bf16[1,8,8,128]{3,2,1,0:T(8,128)(2,1)S(1)}, u32[]{:S(2)}, u32[]{:S(2)}) %collective-permute-start.5) | collective-permute-done | bytes 16416 | tf_op jit(solution)/shard_map/ppermute | solution.py:240
  25.6 0.6 %add_bitcast_fusion = f32[8,8,128]{2,1,0:T(8,128)} fusion(bf16[1,8,8,128]{3,2,1,0:T(8,128)(2,1)S(1)} %collective-permute-done.5, f32[2,8,8,128]{3,2,1,0:T(8,128)S(1)} %fusion.1, s32[]{:T(128)S(6)} %select_n.34), kind=kLoop, calls=%fused_computation.10 | loop fusion | flops 16384 | bytes 81924 | tf_op jit(solution)/shard_map/squeeze | solution.py:250
  (4 shorter events, 0.1 us)
Async XLA Ops:
  5.2 6.5 %collective-permute-start = (bf16[8,64,128]{2,1,0:T(8,128)(2,1)S(1)}, bf16[8,64,128]{2,1,0:T(8,128)(2,1)S(1)}, u32[]{:S(2)}, u32[]{:S(2)}) collective-permute-start(bf16[8,64,128]{2,1,0:T(8,128)(2,1)S(1)} %get-tuple-element.14), channel_id=1, source_target_pairs={{0,16},{16,0},{1,17},{17,1},{2,18},{18,2},{3,19},{19,3},{4,20},{20... | collective-permute-start | bytes 393224 | tf_op jit(solution)/shard_map/ppermute | solution.py:215
  8.2 3.5 %copy-start = (bf16[8,128,128]{2,1,0:T(8,128)(2,1)S(1)}, bf16[8,128,128]{2,1,0:T(8,128)(2,1)}, u32[]{:S(2)}) copy-start(bf16[8,128,128]{2,1,0:T(8,128)(2,1)} %refs_1_.3) | copy-start | bytes 786436
  8.2 3.5 %copy-start.1 = (bf16[8,64,128]{2,1,0:T(8,128)(2,1)S(1)}, bf16[8,64,128]{2,1,0:T(8,128)(2,1)}, u32[]{:S(2)}) copy-start(bf16[8,64,128]{2,1,0:T(8,128)(2,1)} %refs_2_.3) | copy-start | bytes 393220
  12.1 1.4 %collective-permute-start.1 = (bf16[8,8,8,128]{3,2,1,0:T(8,128)(2,1)S(1)}, bf16[8,8,8,128]{3,2,1,0:T(8,128)(2,1)S(1)}, u32[]{:S(2)}, u32[]{:S(2)}) collective-permute-start(bf16[8,8,8,128]{3,2,1,0:T(8,128)(2,1)S(1)} %get-tuple-element.17), channel_id=1, source_target_pairs={{0,1},{1,0},{2,3},{3,2},{4,5},{5,4},{6,7},{7,6},{8,9},{9,8},{10,11... | collective-permute-start | bytes 393224 | tf_op jit(solution)/shard_map/ppermute | solution.py:240
  13.6 4.9 %collective-permute-start.4 = (bf16[2,8,8,128]{3,2,1,0:T(8,128)(2,1)S(1)}, bf16[2,8,8,128]{3,2,1,0:T(8,128)(2,1)S(1)}, u32[]{:S(2)}, u32[]{:S(2)}) collective-permute-start(bf16[2,8,8,128]{3,2,1,0:T(8,128)(2,1)S(1)} %get-tuple-element.20), channel_id=1, source_target_pairs={{0,6},{1,7},{2,4},{3,5},{4,2},{5,3},{6,0},{7,1},{8,14},{9,15},{10,... | collective-permute-start | bytes 98312 | tf_op jit(solution)/shard_map/ppermute | solution.py:240
  16.5 3.9 %collective-permute-start.3 = (bf16[2,8,8,128]{3,2,1,0:T(8,128)(2,1)S(1)}, bf16[2,8,8,128]{3,2,1,0:T(8,128)(2,1)S(1)}, u32[]{:S(2)}, u32[]{:S(2)}) collective-permute-start(bf16[2,8,8,128]{3,2,1,0:T(8,128)(2,1)S(1)} %get-tuple-element.19), channel_id=1, source_target_pairs={{0,4},{1,5},{2,6},{3,7},{4,0},{5,1},{6,2},{7,3},{8,12},{9,13},{10,... | collective-permute-start | bytes 98312 | tf_op jit(solution)/shard_map/ppermute | solution.py:240
  16.9 3.9 %collective-permute-start.2 = (bf16[2,8,8,128]{3,2,1,0:T(8,128)(2,1)S(1)}, bf16[2,8,8,128]{3,2,1,0:T(8,128)(2,1)S(1)}, u32[]{:S(2)}, u32[]{:S(2)}) collective-permute-start(bf16[2,8,8,128]{3,2,1,0:T(8,128)(2,1)S(1)} %get-tuple-element.18), channel_id=1, source_target_pairs={{0,2},{1,3},{2,0},{3,1},{4,6},{5,7},{6,4},{7,5},{8,10},{9,11},{10,... | collective-permute-start | bytes 98312 | tf_op jit(solution)/shard_map/ppermute | solution.py:240
  20.9 4.7 %collective-permute-start.5 = (bf16[1,8,8,128]{3,2,1,0:T(8,128)(2,1)S(1)}, bf16[1,8,8,128]{3,2,1,0:T(8,128)(2,1)S(1)}, u32[]{:S(2)}, u32[]{:S(2)}) collective-permute-start(bf16[1,8,8,128]{3,2,1,0:T(8,128)(2,1)S(1)} %dynamic-slice_convert_fusion), channel_id=1, source_target_pairs={{0,8},{1,9},{2,10},{3,11},{4,12},{5,13},{6,14},{7,15},{8,0},{9,1},... | collective-permute-start | bytes 49160 | tf_op jit(solution)/shard_map/ppermute | solution.py:240

commit v6 on v5

--- a/solution.py
+++ b/solution.py
@@ -14,7 +14,7 @@
 VMEM = pl.BlockSpec(memory_space=pltpu.VMEM)
 HBM = pl.BlockSpec(memory_space=pltpu.HBM)
 SKEW = 16
-CHUNKS = 2
+CUTS = (1, 1, 2)
 VMEM_LIMIT = 28 * 2**20
 
 
@@ -30,33 +30,39 @@
 
 def decode_kernel(*refs, step, first):
     if first:
-        (vib, hadamard, pilots, owner, live, records), (out, held, signs_v, ordered, weight) = refs[:6], refs[6:11]
-        mix, skewed, mixed, shifted, sems, vib_s, pilots_v, owner_v, live_v, backward = refs[11:]
-    else:
-        held, signs_v, ordered, out, mix, skewed, mixed, shifted = refs
+        (vib, hadamard, pilots, records), (out, held, signs_v, backward) = refs[:4], refs[4:8]
+        mix, skewed, mixed, shifted, sems, vib_s, pilots_v = refs[8:]
+    else:
+        (vib, owner, live, held, signs_v, backward), (out, weight) = refs[:6], refs[6:8]
+        mix, skewed, mixed, shifted, sems, vib_s = refs[8:]
     sweeps, channels, samples = held.shape
     owned, _, lags = out.shape
     all_sweeps, codes = signs_v.shape
     block = mix.shape[1] // sweeps
     shift = block.bit_length() - 1
     early = shifted.shape[0]
-    width = samples // CHUNKS
+    bounds = [samples * sum(CUTS[:k]) // sum(CUTS) for k in range(len(CUTS) + 1)]
     mine = lax.axis_index("sweep")
     first_sweep = mine * sweeps
     first_code = lax.rem(mine + step, lax.axis_size("sweep")) * owned
 
     def fetch(k):
-        cols = pl.ds(k * width, width)
+        cols = pl.ds(bounds[k], bounds[k + 1] - bounds[k])
         return pltpu.make_async_copy(records.at[:, :, cols], held.at[:, :, cols], sems.at[k])
 
     if first:
-        small = [(hadamard, signs_v), (pilots, pilots_v), (vib, vib_s), (owner, owner_v), (live, live_v)]
-        small = [pltpu.make_async_copy(x, y, sems.at[CHUNKS + i]) for i, (x, y) in enumerate(small)]
+        small = [(hadamard, signs_v), (pilots, pilots_v), (vib, vib_s)]
+        small = [pltpu.make_async_copy(x, y, sems.at[len(CUTS) + i]) for i, (x, y) in enumerate(small)]
         for copy in small:
             copy.start()
-        for k in range(CHUNKS):
+        for k in range(len(CUTS)):
             fetch(k).start()
-        small[0].wait()
+        for copy in small:
+            copy.wait()
+
+    else:
+        copy = pltpu.make_async_copy(vib, vib_s, sems.at[0])
+        copy.start()
 
     signs = signs_v[...].astype(F32).astype(BF16)
     rows, cols = mix.shape
@@ -68,7 +74,6 @@
     mix[...] = jnp.where(same, spread, 0.0).astype(BF16)
 
     if first:
-        small[1].wait()
         vibrators, length = pilots.shape
         flip = (iota((lags, lags), 0) + iota((lags, lags), 1) == lags - 1).astype(F32).astype(BF16)
         pieces = jnp.concatenate([pilots_v[:, j : j + lags] for j in range(0, length, lags)], axis=0)
@@ -79,21 +84,14 @@
             backward[:, j * lags : (j + 1) * lags] = (
                 pieces[source : source + vibrators] if inside else jnp.zeros((vibrators, lags), F32)
             )
-        small[2].wait()
-        for c in range(codes):
-            ordered[pl.ds(c, 1), :] = backward[pl.ds(vib_s[c], 1), :]
-        small[3].wait()
-        small[4].wait()
-        owner_c, live_c = column(owner_v[...]), column(live_v[...])
-        for c in range(owned):
-            match = (owner_c == vib_s[mine * owned + c].astype(F32)).astype(F32)
-            weight[c] = jnp.broadcast_to(live_c * (0.25 + match), weight.shape[1:])
+    else:
+        copy.wait()
     made = 0
 
     def skew(upto):
         nonlocal made
         while made < min(upto, owned):
-            row = ordered[pl.ds(first_code + made, 1), :]
+            row = backward[pl.ds(vib_s[first_code + made], 1), :]
             wide = jnp.broadcast_to(row, (SKEW, samples + lags))
             skewed[made] = pltpu.roll(wide, 1, 1, stride=1, stride_axis=0).astype(BF16)
             made += 1
@@ -105,21 +103,28 @@
         )
 
     skew(2)
-    for k in range(CHUNKS):
+    cuts = bounds if first else [0, samples // 2, samples]
+    for k in range(len(cuts) - 1):
+        start, stop = cuts[k], cuts[k + 1]
         if first:
             fetch(k).wait()
-        for c in range(early * k // CHUNKS, early * (k + 1) // CHUNKS):
+        for c in range(early * start // samples, early * stop // samples):
             skew(c + 1)
             shifted[c] = shifts(c)
-        skew(2 + (owned - 2) * (k + 1) // CHUNKS)
+        skew(2 + (owned - 2) * stop // samples)
         for h in range(0, channels, block):
-            traces = held[:, h : h + block, k * width : (k + 1) * width].reshape(cols, width)
+            traces = held[:, h : h + block, start:stop].reshape(cols, stop - start)
             lines = jnp.dot(mix[...], traces, preferred_element_type=F32).astype(BF16)
             for c in range(owned):
-                mixed[c, h : h + block, k * width : (k + 1) * width] = lines[c * block : (c + 1) * block]
+                mixed[c, h : h + block, start:stop] = lines[c * block : (c + 1) * block]
     for c in range(owned):
         kernel = shifted[c] if c < early else shifts(c)
         out[c] = jnp.dot(mixed[c], kernel, preferred_element_type=F32).astype(out.dtype)
+    if not first:
+        owner_c, live_c = column(owner[...]), column(live[...])
+        for c in range(owned):
+            match = (owner_c == vib_s[first_code + c].astype(F32)).astype(F32)
+            weight[c] = jnp.broadcast_to(live_c * (0.25 + match), weight.shape[1:])
 
 
 def decode(inputs, shape, owned, codes, lags, step, dtype, first):
@@ -133,27 +138,30 @@
         pltpu.VMEM((owned, channels, samples), BF16),
         pltpu.VMEM((early, samples, lags), BF16),
     ]
-    if first:
-        vib, hadamard, pilots, owner, live, _ = inputs
+    vib = inputs[0]
+    if first:
+        _, hadamard, pilots, _ = inputs
         inputs = [pltpu.with_memory_space_constraint(x, pltpu.HBM) for x in inputs]
+        specs = [HBM] * 4
         out_shape += [
             pltpu.VMEM(shape, BF16),
             pltpu.VMEM(hadamard.shape, jnp.int32),
-            pltpu.VMEM((codes, samples + lags), F32),
-            pltpu.VMEM((owned, channels, lags), F32),
+            pltpu.VMEM((pilots.shape[0], samples + lags), F32),
         ]
         scratch += [
-            pltpu.SemaphoreType.DMA((CHUNKS + 5,)),
+            pltpu.SemaphoreType.DMA((len(CUTS) + 3,)),
             pltpu.SMEM(vib.shape, jnp.int32),
             pltpu.VMEM(pilots.shape, BF16),
-            pltpu.VMEM(owner.shape, jnp.int32),
-            pltpu.VMEM(live.shape, jnp.int32),
-            pltpu.VMEM((pilots.shape[0], samples + lags), F32),
         ]
+    else:
+        inputs = [pltpu.with_memory_space_constraint(vib, pltpu.HBM), *inputs[1:]]
+        specs = [HBM] + [VMEM] * (len(inputs) - 1)
+        out_shape += [pltpu.VMEM((owned, channels, lags), F32)]
+        scratch += [pltpu.SemaphoreType.DMA((1,)), pltpu.SMEM(vib.shape, jnp.int32)]
     return pl.pallas_call(
         functools.partial(decode_kernel, step=step, first=first),
         out_shape=out_shape,
-        in_specs=[HBM if first else VMEM] * len(inputs),
+        in_specs=specs,
         out_specs=[VMEM] * len(out_shape),
         scratch_shapes=scratch,
         compiler_params=pltpu.CompilerParams(vmem_limit_bytes=VMEM_LIMIT),
@@ -203,16 +211,18 @@
     owned, lags, _ = filters.shape
     channels = records.shape[1]
     received = []
-    inputs = (code_vibrator, hadamard, pilots, owner_map.reshape(1, channels), live_mask.reshape(1, channels), records)
+    inputs = (code_vibrator, hadamard, pilots, records)
     first = True
     for step in list(range(1, groups)) + [0]:
         dtype = BF16 if step else F32
         part, *extra = decode(inputs, records.shape, owned, codes, lags, step, dtype, first)
         if first:
-            *inputs, weight = extra
+            row = (1, channels)
+            inputs = (code_vibrator, owner_map.reshape(row), live_mask.reshape(row), *extra)
             first = False
         if step:
             received.append(lax.ppermute(part, "sweep", [(i, (i + step) % groups) for i in range(groups)]))
+    weight = extra[0]
     share_rows = lags // size
     radices = rounds(size)
     piece = (size // radices[0], owned, share_rows, lags)

time: 26.4 us -> 26.2 us (level)
  waiting for transfers between devices: 6.95 us -> 6.07 us
  Pallas kernels: 7.8 us -> 8.5 us
    pallas_call x2, Pallas kernels: 7.4 us -> 8.1 us  [decode(): pl.pallas_call(functools.partial(decode_kernel, step=step, first=first),...]
    ppermute x1, waiting for transfers between devices: 0.64 us -> 0.01 us  [local(): lax.ppermute(part, 'sweep', [(i, (i + step) % groups) for i in range(grou...]
    unnamed x5 -> x9, local copies, waits for them, and re-layouts: 0.71 us -> 0.72 us
  transfers between devices with their start and end apart: 6 -> 6, of which waited for: 6 -> 5; matrix products, arithmetic and copies ran while one was open for 3% -> 3% of each run, Pallas kernels for 11% -> 14%
where the time goes in v6:
time: 26.2 us; the launch traced here: 26.1 us
  starting transfers between devices  9.31 us (36%)
  Pallas kernels  8.5 us (32%)
  waiting for transfers between devices  6.07 us (23%)
  between operations  0.77 us (3%)
  local copies, waits for them, and re-layouts  0.76 us (3%)
  other arithmetic  0.66 us (3%)
    pallas_call x2, Pallas kernels, decode(): pl.pallas_call(functools.partial(decode_kernel, step=step, first=first),...  8.1 us
    ppermute x5, starting transfers between devices, local(): held = held + lax.ppermute(value, 'recv', pairs).astype(F32)  6.27 us
    ppermute x5, waiting for transfers between devices, local(): held = held + lax.ppermute(value, 'recv', pairs).astype(F32)  6.07 us
    ppermute x1, starting transfers between devices, local(): lax.ppermute(part, 'sweep', [(i, (i + step) % groups) for i in range(grou...  3.04 us
    unnamed x9, local copies, waits for them, and re-layouts  0.72 us
    squeeze x1, other arithmetic, local(): return (responses, held[0])  0.62 us
  transfers between devices with their start and end apart: 6, of which 5 were waited for; matrix products, arithmetic and copies ran while one was open for 3% of the time, Pallas kernels for 14%

profile of v6, /device:TPU:0, one launch (start us, length us, event | category | flops | bytes accessed | tf_op | source)
XLA Modules:
  0.0 26.1 jit_solution(3147551772607795733)
XLA Ops:
  0.6 0.0 copy-start.2
  0.6 0.0 copy-start.3
  0.7 4.4 %decode_1.1 = (bf16[8,64,128]{2,1,0:T(8,128)(2,1)S(1)}, bf16[8,64,4096]{2,1,0:T(8,128)(2,1)S(1)}, s32[16,16]{1,0:T(8,128)S(1)}, f32[16,4224]{1,0:T(8,128)S(1)}) custom-call(s32[16]{0:T(128)} %refs_0_.3, s32[16,16]{1,0:T(8,128)} %refs_1_.2, bf16[16,3968]{1,0:T(8,128)(2,1)} %refs_2_.2, bf16[8,64,4096]{2,1,0:T(8,128)(2,1)} %refs_3_.1), custom_call_target="tpu_custom_call" | custom-call | flops 8000000000 | bytes 4194304 | tf_op jit(solution)/shard_map/decode_1/pallas_call | solution.py:161
  5.1 3.0 %collective-permute-start = (bf16[8,64,128]{2,1,0:T(8,128)(2,1)S(1)}, bf16[8,64,128]{2,1,0:T(8,128)(2,1)S(1)}, u32[]{:S(2)}, u32[]{:S(2)}) collective-permute-start(bf16[8,64,128]{2,1,0:T(8,128)(2,1)S(1)} %get-tuple-element.16), channel_id=1, source_target_pairs={{0,16},{16,0},{1,17},{17,1},{2,18},{18,2},{3,19},{19,3},{4,20},{20... | collective-permute-start | bytes 393224 | tf_op jit(solution)/shard_map/ppermute | solution.py:224
  8.1 0.0 copy-done.2
  8.1 0.0 copy-done.3
  8.1 0.0 copy-start
  8.1 0.0 copy-start.1
  8.1 3.7 %decode_0.1 = (f32[8,64,128]{2,1,0:T(8,128)S(1)}, f32[8,64,128]{2,1,0:T(8,128)S(1)}) custom-call(s32[16]{0:T(128)} %refs_0_.3, s32[1,64]{1,0:T(1,128)S(1)} %bitcast.29, s32[1,64]{1,0:T(1,128)S(1)} %bitcast.30, bf16[8,64,4096]{2,1,0:T(8,128)(2,1)S(1)} %get-tuple-element.11.refs_3_, s32[16,16]{1,0:T(8,128)S(1)} %get-tuple-element.12.refs_4_, ...), custom_call_target="tpu_custom_call" | custom-call | flops 8000000000 | bytes 4194304 | tf_op jit(solution)/shard_map/decode_0/pallas_call | solution.py:161
  11.8 0.0 collective-permute-done.refs_0_
  11.8 0.0 copy-done
  11.8 0.0 copy-done.1
  11.8 0.4 %tail.1 = (f32[8,64,128]{2,1,0:T(8,128)S(1)}, f32[8,8,8,128]{3,2,1,0:T(8,128)S(1)}, bf16[8,8,8,128]{3,2,1,0:T(8,128)(2,1)S(1)}) custom-call(f32[8,64,128]{2,1,0:T(8,128)S(1)} %get-tuple-element.14.weight, f32[8,64,128]{2,1,0:T(8,128)S(1)} %get-tuple-element.15.own, bf16[8,64,128]{2,1,0:T(8,128)(2,1)S(1)} %collective-permute-done.refs_0_, ...), custom_call_target="tpu_custom_call" | custom-call | tf_op jit(solution)/shard_map/tail/pallas_call | solution.py:229
  12.3 0.1 collective-permute-start.1
  12.4 1.3 %collective-permute-done.1 = bf16[8,8,8,128]{3,2,1,0:T(8,128)(2,1)S(1)} collective-permute-done((bf16[8,8,8,128]{3,2,1,0:T(8,128)(2,1)S(1)}, bf16[8,8,8,128]{3,2,1,0:T(8,128)(2,1)S(1)}, u32[]{:S(2)}, u32[]{:S(2)}) %collective-permute-start.1) | collective-permute-done | bytes 131104 | tf_op jit(solution)/shard_map/ppermute | solution.py:250
  13.7 2.6 %collective-permute-start.4 = (bf16[2,8,8,128]{3,2,1,0:T(8,128)(2,1)S(1)}, bf16[2,8,8,128]{3,2,1,0:T(8,128)(2,1)S(1)}, u32[]{:S(2)}, u32[]{:S(2)}) collective-permute-start(bf16[2,8,8,128]{3,2,1,0:T(8,128)(2,1)S(1)} %get-tuple-element.22), channel_id=1, source_target_pairs={{0,6},{1,7},{2,4},{3,5},{4,2},{5,3},{6,0},{7,1},{8,14},{9,15},{10,... | collective-permute-start | bytes 98312 | tf_op jit(solution)/shard_map/ppermute | solution.py:250
  16.3 0.5 %collective-permute-start.3 = (bf16[2,8,8,128]{3,2,1,0:T(8,128)(2,1)S(1)}, bf16[2,8,8,128]{3,2,1,0:T(8,128)(2,1)S(1)}, u32[]{:S(2)}, u32[]{:S(2)}) collective-permute-start(bf16[2,8,8,128]{3,2,1,0:T(8,128)(2,1)S(1)} %get-tuple-element.21), channel_id=1, source_target_pairs={{0,4},{1,5},{2,6},{3,7},{4,0},{5,1},{6,2},{7,3},{8,12},{9,13},{10,... | collective-permute-start | bytes 98312 | tf_op jit(solution)/shard_map/ppermute | solution.py:250
  16.8 0.5 %collective-permute-start.2 = (bf16[2,8,8,128]{3,2,1,0:T(8,128)(2,1)S(1)}, bf16[2,8,8,128]{3,2,1,0:T(8,128)(2,1)S(1)}, u32[]{:S(2)}, u32[]{:S(2)}) collective-permute-start(bf16[2,8,8,128]{3,2,1,0:T(8,128)(2,1)S(1)} %get-tuple-element.20), channel_id=1, source_target_pairs={{0,2},{1,3},{2,0},{3,1},{4,6},{5,7},{6,4},{7,5},{8,10},{9,11},{10,... | collective-permute-start | bytes 98312 | tf_op jit(solution)/shard_map/ppermute | solution.py:250
  17.3 1.3 %collective-permute-done.4 = bf16[2,8,8,128]{3,2,1,0:T(8,128)(2,1)S(1)} collective-permute-done((bf16[2,8,8,128]{3,2,1,0:T(8,128)(2,1)S(1)}, bf16[2,8,8,128]{3,2,1,0:T(8,128)(2,1)S(1)}, u32[]{:S(2)}, u32[]{:S(2)}) %collective-permute-start.4) | collective-permute-done | bytes 32800 | tf_op jit(solution)/shard_map/ppermute | solution.py:250
  18.6 1.6 %collective-permute-done.3 = bf16[2,8,8,128]{3,2,1,0:T(8,128)(2,1)S(1)} collective-permute-done((bf16[2,8,8,128]{3,2,1,0:T(8,128)(2,1)S(1)}, bf16[2,8,8,128]{3,2,1,0:T(8,128)(2,1)S(1)}, u32[]{:S(2)}, u32[]{:S(2)}) %collective-permute-start.3) | collective-permute-done | bytes 32800 | tf_op jit(solution)/shard_map/ppermute | solution.py:250
  20.2 0.5 %collective-permute-done.2 = bf16[2,8,8,128]{3,2,1,0:T(8,128)(2,1)S(1)} collective-permute-done((bf16[2,8,8,128]{3,2,1,0:T(8,128)(2,1)S(1)}, bf16[2,8,8,128]{3,2,1,0:T(8,128)(2,1)S(1)}, u32[]{:S(2)}, u32[]{:S(2)}) %collective-permute-start.2) | collective-permute-done | bytes 32800 | tf_op jit(solution)/shard_map/ppermute | solution.py:250
  20.7 2.6 %collective-permute-start.5 = (bf16[1,8,8,128]{3,2,1,0:T(8,128)(2,1)S(1)}, bf16[1,8,8,128]{3,2,1,0:T(8,128)(2,1)S(1)}, u32[]{:S(2)}, u32[]{:S(2)}) collective-permute-start(bf16[1,8,8,128]{3,2,1,0:T(8,128)(2,1)S(1)} %dynamic-slice_convert_fusion), channel_id=1, source_target_pairs={{0,8},{1,9},{2,10},{3,11},{4,12},{5,13},{6,14},{7,15},{8,0},{9,1},... | collective-permute-start | bytes 49160 | tf_op jit(solution)/shard_map/ppermute | solution.py:250
  23.4 0.7 %copy.16 = f32[8,64,128]{2,1,0:T(8,128)} copy(f32[8,64,128]{2,1,0:T(8,128)S(1)} %get-tuple-element.23) | data formatting | bytes 524288
  24.1 1.4 %collective-permute-done.5 = bf16[1,8,8,128]{3,2,1,0:T(8,128)(2,1)S(1)} collective-permute-done((bf16[1,8,8,128]{3,2,1,0:T(8,128)(2,1)S(1)}, bf16[1,8,8,128]{3,2,1,0:T(8,128)(2,1)S(1)}, u32[]{:S(2)}, u32[]{:S(2)}) %collective-permute-start.5) | collective-permute-done | bytes 16416 | tf_op jit(solution)/shard_map/ppermute | solution.py:250
  25.4 0.6 %add_bitcast_fusion = f32[8,8,128]{2,1,0:T(8,128)} fusion(bf16[1,8,8,128]{3,2,1,0:T(8,128)(2,1)S(1)} %collective-permute-done.5, f32[2,8,8,128]{3,2,1,0:T(8,128)S(1)} %fusion.1, s32[]{:T(128)S(6)} %select_n.34), kind=kLoop, calls=%fused_computation.10 | loop fusion | flops 16384 | bytes 81924 | tf_op jit(solution)/shard_map/squeeze | solution.py:260
  (4 shorter events, 0.1 us)
Async XLA Ops:
  0.6 7.5 %copy-start.2 = (s32[64]{0:T(128)S(1)}, s32[64]{0:T(128)}, u32[]{:S(2)}) copy-start(s32[64]{0:T(128)} %param.12) | copy-start | bytes 772
  0.6 7.5 %copy-start.3 = (s32[64]{0:T(128)S(1)}, s32[64]{0:T(128)}, u32[]{:S(2)}) copy-start(s32[64]{0:T(128)} %param.13) | copy-start | bytes 772
  5.1 6.8 %collective-permute-start = (bf16[8,64,128]{2,1,0:T(8,128)(2,1)S(1)}, bf16[8,64,128]{2,1,0:T(8,128)(2,1)S(1)}, u32[]{:S(2)}, u32[]{:S(2)}) collective-permute-start(bf16[8,64,128]{2,1,0:T(8,128)(2,1)S(1)} %get-tuple-element.16), channel_id=1, source_target_pairs={{0,16},{16,0},{1,17},{17,1},{2,18},{18,2},{3,19},{19,3},{4,20},{20... | collective-permute-start | bytes 393224 | tf_op jit(solution)/shard_map/ppermute | solution.py:224
  8.1 3.7 %copy-start = (bf16[8,128,128]{2,1,0:T(8,128)(2,1)S(1)}, bf16[8,128,128]{2,1,0:T(8,128)(2,1)}, u32[]{:S(2)}) copy-start(bf16[8,128,128]{2,1,0:T(8,128)(2,1)} %refs_1_.3) | copy-start | bytes 786436
  8.1 3.7 %copy-start.1 = (bf16[8,64,128]{2,1,0:T(8,128)(2,1)S(1)}, bf16[8,64,128]{2,1,0:T(8,128)(2,1)}, u32[]{:S(2)}) copy-start(bf16[8,64,128]{2,1,0:T(8,128)(2,1)} %refs_2_.3) | copy-start | bytes 393220
  12.3 1.4 %collective-permute-start.1 = (bf16[8,8,8,128]{3,2,1,0:T(8,128)(2,1)S(1)}, bf16[8,8,8,128]{3,2,1,0:T(8,128)(2,1)S(1)}, u32[]{:S(2)}, u32[]{:S(2)}) collective-permute-start(bf16[8,8,8,128]{3,2,1,0:T(8,128)(2,1)S(1)} %get-tuple-element.19), channel_id=1, source_target_pairs={{0,1},{1,0},{2,3},{3,2},{4,5},{5,4},{6,7},{7,6},{8,9},{9,8},{10,11... | collective-permute-start | bytes 393224 | tf_op jit(solution)/shard_map/ppermute | solution.py:250
  13.7 4.9 %collective-permute-start.4 = (bf16[2,8,8,128]{3,2,1,0:T(8,128)(2,1)S(1)}, bf16[2,8,8,128]{3,2,1,0:T(8,128)(2,1)S(1)}, u32[]{:S(2)}, u32[]{:S(2)}) collective-permute-start(bf16[2,8,8,128]{3,2,1,0:T(8,128)(2,1)S(1)} %get-tuple-element.22), channel_id=1, source_target_pairs={{0,6},{1,7},{2,4},{3,5},{4,2},{5,3},{6,0},{7,1},{8,14},{9,15},{10,... | collective-permute-start | bytes 98312 | tf_op jit(solution)/shard_map/ppermute | solution.py:250
  16.3 3.9 %collective-permute-start.3 = (bf16[2,8,8,128]{3,2,1,0:T(8,128)(2,1)S(1)}, bf16[2,8,8,128]{3,2,1,0:T(8,128)(2,1)S(1)}, u32[]{:S(2)}, u32[]{:S(2)}) collective-permute-start(bf16[2,8,8,128]{3,2,1,0:T(8,128)(2,1)S(1)} %get-tuple-element.21), channel_id=1, source_target_pairs={{0,4},{1,5},{2,6},{3,7},{4,0},{5,1},{6,2},{7,3},{8,12},{9,13},{10,... | collective-permute-start | bytes 98312 | tf_op jit(solution)/shard_map/ppermute | solution.py:250
  16.8 3.9 %collective-permute-start.2 = (bf16[2,8,8,128]{3,2,1,0:T(8,128)(2,1)S(1)}, bf16[2,8,8,128]{3,2,1,0:T(8,128)(2,1)S(1)}, u32[]{:S(2)}, u32[]{:S(2)}) collective-permute-start(bf16[2,8,8,128]{3,2,1,0:T(8,128)(2,1)S(1)} %get-tuple-element.20), channel_id=1, source_target_pairs={{0,2},{1,3},{2,0},{3,1},{4,6},{5,7},{6,4},{7,5},{8,10},{9,11},{10,... | collective-permute-start | bytes 98312 | tf_op jit(solution)/shard_map/ppermute | solution.py:250
  20.7 4.7 %collective-permute-start.5 = (bf16[1,8,8,128]{3,2,1,0:T(8,128)(2,1)S(1)}, bf16[1,8,8,128]{3,2,1,0:T(8,128)(2,1)S(1)}, u32[]{:S(2)}, u32[]{:S(2)}) collective-permute-start(bf16[1,8,8,128]{3,2,1,0:T(8,128)(2,1)S(1)} %dynamic-slice_convert_fusion), channel_id=1, source_target_pairs={{0,8},{1,9},{2,10},{3,11},{4,12},{5,13},{6,14},{7,15},{8,0},{9,1},... | collective-permute-start | bytes 49160 | tf_op jit(solution)/shard_map/ppermute | solution.py:250

commit v7 on v6

--- a/solution.py
+++ b/solution.py
@@ -171,9 +171,9 @@
 
 
 def tail_kernel(weight, own, *refs, parts, norm, factor, radix):
-    others, (filters, targets, responses, keep, *sends, terms) = refs[:parts], refs[parts:]
+    others, (filters, targets, responses, keep, *sends) = refs[:parts], refs[parts:]
     owned = own.shape[0]
-    shares, _, share_rows, _ = terms.shape
+    shares, share_rows = keep.shape[0] * radix, keep.shape[2]
     every = range(owned)
     partial = [own[c] for c in every]
     for other in others:
@@ -187,14 +187,12 @@
         factor * lax.dot_general(decoded[c], residual[c], (((0,), (0,)), ((), ())), preferred_element_type=F32)
         for c in every
     ]
+    odd = lax.rem(lax.axis_index("recv"), radix) == 1
     for c in every:
-        for d in range(shares):
-            terms[d, c] = grad[c][d * share_rows : (d + 1) * share_rows]
-    digit = lax.rem(lax.axis_index("recv"), radix)
-    for i in range(shares // radix):
-        keep[i] = terms[i * radix + digit]
-        for k, send in enumerate(sends):
-            send[i] = terms[i * radix + (digit ^ (k + 1))].astype(BF16)
+        for i in range(shares // radix):
+            low, high = (grad[c][d * share_rows : (d + 1) * share_rows] for d in (2 * i, 2 * i + 1))
+            keep[i, c] = jnp.where(odd, high, low)
+            sends[0][i, c] = jnp.where(odd, low, high).astype(BF16)
 
 
 def rounds(size):
@@ -238,7 +236,6 @@
         + [pltpu.VMEM(piece, BF16)] * (radices[0] - 1),
         in_specs=[VMEM] * (4 + len(received)),
         out_specs=[VMEM] * (1 + radices[0]),
-        scratch_shapes=[pltpu.VMEM((size, owned, share_rows, lags), F32)],
         compiler_params=pltpu.CompilerParams(vmem_limit_bytes=8 * 2**20),
         name="tail",
     )(weight, part, *received, filters, targets)

time: 26.2 us -> 26.2 us (level)
  no operation moved by 1% of the time
where the time goes in v7:
time: 26.2 us; the launch traced here: 26 us
  starting transfers between devices  9.33 us (36%)
  Pallas kernels  8.47 us (32%)
  waiting for transfers between devices  6.04 us (23%)
  local copies, waits for them, and re-layouts  0.76 us (3%)
  between operations  0.76 us (3%)
  other arithmetic  0.66 us (3%)
    pallas_call x2, Pallas kernels, decode(): pl.pallas_call(functools.partial(decode_kernel, step=step, first=first),...  8.1 us
    ppermute x5, starting transfers between devices, local(): held = held + lax.ppermute(value, 'recv', pairs).astype(F32)  6.28 us
    ppermute x5, waiting for transfers between devices, local(): held = held + lax.ppermute(value, 'recv', pairs).astype(F32)  6.04 us
    ppermute x1, starting transfers between devices, local(): lax.ppermute(part, 'sweep', [(i, (i + step) % groups) for i in range(grou...  3.05 us
    unnamed x9, local copies, waits for them, and re-layouts  0.72 us
    squeeze x1, other arithmetic, local(): return (responses, held[0])  0.62 us
  transfers between devices with their start and end apart: 6, of which 5 were waited for; matrix products, arithmetic and copies ran while one was open for 3% of the time, Pallas kernels for 14%

profile of v7, /device:TPU:0, one launch (start us, length us, event | category | flops | bytes accessed | tf_op | source)
XLA Modules:
  0.0 26.0 jit_solution(4862084712424778242)
XLA Ops:
  0.6 0.0 copy-start.2
  0.6 0.0 copy-start.3
  0.7 4.4 %decode_1.1 = (bf16[8,64,128]{2,1,0:T(8,128)(2,1)S(1)}, bf16[8,64,4096]{2,1,0:T(8,128)(2,1)S(1)}, s32[16,16]{1,0:T(8,128)S(1)}, f32[16,4224]{1,0:T(8,128)S(1)}) custom-call(s32[16]{0:T(128)} %refs_0_.3, s32[16,16]{1,0:T(8,128)} %refs_1_.2, bf16[16,3968]{1,0:T(8,128)(2,1)} %refs_2_.2, bf16[8,64,4096]{2,1,0:T(8,128)(2,1)} %refs_3_.1), custom_call_target="tpu_custom_call" | custom-call | flops 8000000000 | bytes 4194304 | tf_op jit(solution)/shard_map/decode_1/pallas_call | solution.py:161
  5.1 3.0 %collective-permute-start = (bf16[8,64,128]{2,1,0:T(8,128)(2,1)S(1)}, bf16[8,64,128]{2,1,0:T(8,128)(2,1)S(1)}, u32[]{:S(2)}, u32[]{:S(2)}) collective-permute-start(bf16[8,64,128]{2,1,0:T(8,128)(2,1)S(1)} %get-tuple-element.16), channel_id=1, source_target_pairs={{0,16},{16,0},{1,17},{17,1},{2,18},{18,2},{3,19},{19,3},{4,20},{20... | collective-permute-start | bytes 393224 | tf_op jit(solution)/shard_map/ppermute | solution.py:222
  8.1 0.0 copy-done.2
  8.1 0.0 copy-done.3
  8.1 0.0 copy-start
  8.1 0.0 copy-start.1
  8.1 3.7 %decode_0.1 = (f32[8,64,128]{2,1,0:T(8,128)S(1)}, f32[8,64,128]{2,1,0:T(8,128)S(1)}) custom-call(s32[16]{0:T(128)} %refs_0_.3, s32[1,64]{1,0:T(1,128)S(1)} %bitcast.29, s32[1,64]{1,0:T(1,128)S(1)} %bitcast.30, bf16[8,64,4096]{2,1,0:T(8,128)(2,1)S(1)} %get-tuple-element.11.refs_3_, s32[16,16]{1,0:T(8,128)S(1)} %get-tuple-element.12.refs_4_, ...), custom_call_target="tpu_custom_call" | custom-call | flops 8000000000 | bytes 4194304 | tf_op jit(solution)/shard_map/decode_0/pallas_call | solution.py:161
  11.8 0.0 collective-permute-done.refs_0_
  11.8 0.0 copy-done
  11.8 0.0 copy-done.1
  11.9 0.4 %tail.1 = (f32[8,64,128]{2,1,0:T(8,128)S(1)}, f32[8,8,8,128]{3,2,1,0:T(8,128)S(1)}, bf16[8,8,8,128]{3,2,1,0:T(8,128)(2,1)S(1)}) custom-call(f32[8,64,128]{2,1,0:T(8,128)S(1)} %get-tuple-element.14.weight, f32[8,64,128]{2,1,0:T(8,128)S(1)} %get-tuple-element.15.own, bf16[8,64,128]{2,1,0:T(8,128)(2,1)S(1)} %collective-permute-done.refs_0_, ...), custom_call_target="tpu_custom_call" | custom-call | tf_op jit(solution)/shard_map/tail/pallas_call | solution.py:227
  12.2 0.1 collective-permute-start.1
  12.3 1.3 %collective-permute-done.1 = bf16[8,8,8,128]{3,2,1,0:T(8,128)(2,1)S(1)} collective-permute-done((bf16[8,8,8,128]{3,2,1,0:T(8,128)(2,1)S(1)}, bf16[8,8,8,128]{3,2,1,0:T(8,128)(2,1)S(1)}, u32[]{:S(2)}, u32[]{:S(2)}) %collective-permute-start.1) | collective-permute-done | bytes 131104 | tf_op jit(solution)/shard_map/ppermute | solution.py:247
  13.7 2.6 %collective-permute-start.4 = (bf16[2,8,8,128]{3,2,1,0:T(8,128)(2,1)S(1)}, bf16[2,8,8,128]{3,2,1,0:T(8,128)(2,1)S(1)}, u32[]{:S(2)}, u32[]{:S(2)}) collective-permute-start(bf16[2,8,8,128]{3,2,1,0:T(8,128)(2,1)S(1)} %get-tuple-element.22), channel_id=1, source_target_pairs={{0,6},{1,7},{2,4},{3,5},{4,2},{5,3},{6,0},{7,1},{8,14},{9,15},{10,... | collective-permute-start | bytes 98312 | tf_op jit(solution)/shard_map/ppermute | solution.py:247
  16.3 0.4 %collective-permute-start.3 = (bf16[2,8,8,128]{3,2,1,0:T(8,128)(2,1)S(1)}, bf16[2,8,8,128]{3,2,1,0:T(8,128)(2,1)S(1)}, u32[]{:S(2)}, u32[]{:S(2)}) collective-permute-start(bf16[2,8,8,128]{3,2,1,0:T(8,128)(2,1)S(1)} %get-tuple-element.21), channel_id=1, source_target_pairs={{0,4},{1,5},{2,6},{3,7},{4,0},{5,1},{6,2},{7,3},{8,12},{9,13},{10,... | collective-permute-start | bytes 98312 | tf_op jit(solution)/shard_map/ppermute | solution.py:247
  16.7 0.5 %collective-permute-start.2 = (bf16[2,8,8,128]{3,2,1,0:T(8,128)(2,1)S(1)}, bf16[2,8,8,128]{3,2,1,0:T(8,128)(2,1)S(1)}, u32[]{:S(2)}, u32[]{:S(2)}) collective-permute-start(bf16[2,8,8,128]{3,2,1,0:T(8,128)(2,1)S(1)} %get-tuple-element.20), channel_id=1, source_target_pairs={{0,2},{1,3},{2,0},{3,1},{4,6},{5,7},{6,4},{7,5},{8,10},{9,11},{10,... | collective-permute-start | bytes 98312 | tf_op jit(solution)/shard_map/ppermute | solution.py:247
  17.3 1.3 %collective-permute-done.4 = bf16[2,8,8,128]{3,2,1,0:T(8,128)(2,1)S(1)} collective-permute-done((bf16[2,8,8,128]{3,2,1,0:T(8,128)(2,1)S(1)}, bf16[2,8,8,128]{3,2,1,0:T(8,128)(2,1)S(1)}, u32[]{:S(2)}, u32[]{:S(2)}) %collective-permute-start.4) | collective-permute-done | bytes 32800 | tf_op jit(solution)/shard_map/ppermute | solution.py:247
  18.6 1.6 %collective-permute-done.3 = bf16[2,8,8,128]{3,2,1,0:T(8,128)(2,1)S(1)} collective-permute-done((bf16[2,8,8,128]{3,2,1,0:T(8,128)(2,1)S(1)}, bf16[2,8,8,128]{3,2,1,0:T(8,128)(2,1)S(1)}, u32[]{:S(2)}, u32[]{:S(2)}) %collective-permute-start.3) | collective-permute-done | bytes 32800 | tf_op jit(solution)/shard_map/ppermute | solution.py:247
  20.2 0.4 %collective-permute-done.2 = bf16[2,8,8,128]{3,2,1,0:T(8,128)(2,1)S(1)} collective-permute-done((bf16[2,8,8,128]{3,2,1,0:T(8,128)(2,1)S(1)}, bf16[2,8,8,128]{3,2,1,0:T(8,128)(2,1)S(1)}, u32[]{:S(2)}, u32[]{:S(2)}) %collective-permute-start.2) | collective-permute-done | bytes 32800 | tf_op jit(solution)/shard_map/ppermute | solution.py:247
  20.7 2.7 %collective-permute-start.5 = (bf16[1,8,8,128]{3,2,1,0:T(8,128)(2,1)S(1)}, bf16[1,8,8,128]{3,2,1,0:T(8,128)(2,1)S(1)}, u32[]{:S(2)}, u32[]{:S(2)}) collective-permute-start(bf16[1,8,8,128]{3,2,1,0:T(8,128)(2,1)S(1)} %dynamic-slice_convert_fusion), channel_id=1, source_target_pairs={{0,8},{1,9},{2,10},{3,11},{4,12},{5,13},{6,14},{7,15},{8,0},{9,1},... | collective-permute-start | bytes 49160 | tf_op jit(solution)/shard_map/ppermute | solution.py:247
  23.4 0.7 %copy.16 = f32[8,64,128]{2,1,0:T(8,128)} copy(f32[8,64,128]{2,1,0:T(8,128)S(1)} %get-tuple-element.23) | data formatting | bytes 524288
  24.1 1.3 %collective-permute-done.5 = bf16[1,8,8,128]{3,2,1,0:T(8,128)(2,1)S(1)} collective-permute-done((bf16[1,8,8,128]{3,2,1,0:T(8,128)(2,1)S(1)}, bf16[1,8,8,128]{3,2,1,0:T(8,128)(2,1)S(1)}, u32[]{:S(2)}, u32[]{:S(2)}) %collective-permute-start.5) | collective-permute-done | bytes 16416 | tf_op jit(solution)/shard_map/ppermute | solution.py:247
  25.4 0.6 %add_bitcast_fusion = f32[8,8,128]{2,1,0:T(8,128)} fusion(bf16[1,8,8,128]{3,2,1,0:T(8,128)(2,1)S(1)} %collective-permute-done.5, f32[2,8,8,128]{3,2,1,0:T(8,128)S(1)} %fusion.1, s32[]{:T(128)S(6)} %select_n.34), kind=kLoop, calls=%fused_computation.10 | loop fusion | flops 16384 | bytes 81924 | tf_op jit(solution)/shard_map/squeeze | solution.py:257
  (4 shorter events, 0.1 us)
Async XLA Ops:
  0.6 7.5 %copy-start.2 = (s32[64]{0:T(128)S(1)}, s32[64]{0:T(128)}, u32[]{:S(2)}) copy-start(s32[64]{0:T(128)} %param.12) | copy-start | bytes 772
  0.6 7.5 %copy-start.3 = (s32[64]{0:T(128)S(1)}, s32[64]{0:T(128)}, u32[]{:S(2)}) copy-start(s32[64]{0:T(128)} %param.13) | copy-start | bytes 772
  5.1 6.8 %collective-permute-start = (bf16[8,64,128]{2,1,0:T(8,128)(2,1)S(1)}, bf16[8,64,128]{2,1,0:T(8,128)(2,1)S(1)}, u32[]{:S(2)}, u32[]{:S(2)}) collective-permute-start(bf16[8,64,128]{2,1,0:T(8,128)(2,1)S(1)} %get-tuple-element.16), channel_id=1, source_target_pairs={{0,16},{16,0},{1,17},{17,1},{2,18},{18,2},{3,19},{19,3},{4,20},{20... | collective-permute-start | bytes 393224 | tf_op jit(solution)/shard_map/ppermute | solution.py:222
  8.1 3.7 %copy-start = (bf16[8,128,128]{2,1,0:T(8,128)(2,1)S(1)}, bf16[8,128,128]{2,1,0:T(8,128)(2,1)}, u32[]{:S(2)}) copy-start(bf16[8,128,128]{2,1,0:T(8,128)(2,1)} %refs_1_.3) | copy-start | bytes 786436
  8.1 3.7 %copy-start.1 = (bf16[8,64,128]{2,1,0:T(8,128)(2,1)S(1)}, bf16[8,64,128]{2,1,0:T(8,128)(2,1)}, u32[]{:S(2)}) copy-start(bf16[8,64,128]{2,1,0:T(8,128)(2,1)} %refs_2_.3) | copy-start | bytes 393220
  12.2 1.4 %collective-permute-start.1 = (bf16[8,8,8,128]{3,2,1,0:T(8,128)(2,1)S(1)}, bf16[8,8,8,128]{3,2,1,0:T(8,128)(2,1)S(1)}, u32[]{:S(2)}, u32[]{:S(2)}) collective-permute-start(bf16[8,8,8,128]{3,2,1,0:T(8,128)(2,1)S(1)} %get-tuple-element.19), channel_id=1, source_target_pairs={{0,1},{1,0},{2,3},{3,2},{4,5},{5,4},{6,7},{7,6},{8,9},{9,8},{10,11... | collective-permute-start | bytes 393224 | tf_op jit(solution)/shard_map/ppermute | solution.py:247
  13.7 4.9 %collective-permute-start.4 = (bf16[2,8,8,128]{3,2,1,0:T(8,128)(2,1)S(1)}, bf16[2,8,8,128]{3,2,1,0:T(8,128)(2,1)S(1)}, u32[]{:S(2)}, u32[]{:S(2)}) collective-permute-start(bf16[2,8,8,128]{3,2,1,0:T(8,128)(2,1)S(1)} %get-tuple-element.22), channel_id=1, source_target_pairs={{0,6},{1,7},{2,4},{3,5},{4,2},{5,3},{6,0},{7,1},{8,14},{9,15},{10,... | collective-permute-start | bytes 98312 | tf_op jit(solution)/shard_map/ppermute | solution.py:247
  16.3 3.9 %collective-permute-start.3 = (bf16[2,8,8,128]{3,2,1,0:T(8,128)(2,1)S(1)}, bf16[2,8,8,128]{3,2,1,0:T(8,128)(2,1)S(1)}, u32[]{:S(2)}, u32[]{:S(2)}) collective-permute-start(bf16[2,8,8,128]{3,2,1,0:T(8,128)(2,1)S(1)} %get-tuple-element.21), channel_id=1, source_target_pairs={{0,4},{1,5},{2,6},{3,7},{4,0},{5,1},{6,2},{7,3},{8,12},{9,13},{10,... | collective-permute-start | bytes 98312 | tf_op jit(solution)/shard_map/ppermute | solution.py:247
  16.7 3.9 %collective-permute-start.2 = (bf16[2,8,8,128]{3,2,1,0:T(8,128)(2,1)S(1)}, bf16[2,8,8,128]{3,2,1,0:T(8,128)(2,1)S(1)}, u32[]{:S(2)}, u32[]{:S(2)}) collective-permute-start(bf16[2,8,8,128]{3,2,1,0:T(8,128)(2,1)S(1)} %get-tuple-element.20), channel_id=1, source_target_pairs={{0,2},{1,3},{2,0},{3,1},{4,6},{5,7},{6,4},{7,5},{8,10},{9,11},{10,... | collective-permute-start | bytes 98312 | tf_op jit(solution)/shard_map/ppermute | solution.py:247
  20.7 4.7 %collective-permute-start.5 = (bf16[1,8,8,128]{3,2,1,0:T(8,128)(2,1)S(1)}, bf16[1,8,8,128]{3,2,1,0:T(8,128)(2,1)S(1)}, u32[]{:S(2)}, u32[]{:S(2)}) collective-permute-start(bf16[1,8,8,128]{3,2,1,0:T(8,128)(2,1)S(1)} %dynamic-slice_convert_fusion), channel_id=1, source_target_pairs={{0,8},{1,9},{2,10},{3,11},{4,12},{5,13},{6,14},{7,15},{8,0},{9,1},... | collective-permute-start | bytes 49160 | tf_op jit(solution)/shard_map/ppermute | solution.py:247
